TPU v7x, 256 devices: a whole 4x4x8 slice. The times are simulated.
256 devices in a mesh: row: 16 (over z_lo, x), col: 16 (over y, z_hi, core).
Axes of the slice: x: 4, y: 4, z: 8 (z_hi: 2, z_lo: 4; z = z_hi * 4 + z_lo), core: 2. Of those that a mesh axis runs over, the one named last changes fastest.
Arguments:
- homolog_matrix: bfloat16 [128, 1280, 64], P('row', 'col'), may hold values from -6 to 6
- contact_matrix: bfloat16 [1280, 1280, 128], P('row', 'col'), may hold values from -24 to 24
- genuine_homolog_total: int32 [1], replicated, may hold values from 1 to 128
- genuine_chain_length: int32 [1], replicated, may hold values from 640 to 1280
- tensor_product_matrices: bfloat16 [1, 64, 64], replicated, may hold values from -0.75 to 0.75
- tensor_product_final: bfloat16 [1, 1024, 128], replicated, may hold values from -0.75 to 0.75
- mixing_value_gate_matrix: bfloat16 [1, 64, 512], replicated, may hold values from -0.75 to 0.75
- mixing_logit_matrix: bfloat16 [1, 128, 8], replicated
- mixing_final_matrix: bfloat16 [1, 256, 64], replicated, may hold values from -1.5 to 1.5
- feedforward_gate_expand: bfloat16 [1, 128, 1024], replicated, may hold values from -0.5 to 0.5
- feedforward_shrink_matrix: bfloat16 [1, 512, 128], replicated, may hold values from -0.25 to 0.25
Outputs:
- msa_out: bfloat16 [128, 1280, 64], P('row', 'col')
- pair_out: bfloat16 [1280, 1280, 128], P('row', 'col')
Inputs may be any that keep to these rules, and one draw needn't show every extreme that they name: Sequences from genuine_homolog_total on are padding. Residues from genuine_chain_length on are padding.
All inputs are finite; a program needn't handle non-finite values.
Results may differ from a plain program's by a relative error of at most 0.0065.
The roundings to bfloat16 on the way count: a program that leaves them out, or rounds other values in their place, can miss the bound.
Values may be sent and summed in bfloat16 or wider, within the bound.
No kernel may reach another device: no remote copies, remote signals or barrier semaphores. Data moves between devices by JAX's collectives and lax.ppermute only.
A program may use at most 64 MiB of HBM per device.

v0:
```python
import jax
import jax.numpy as jnp
from jax import lax
from jax.sharding import PartitionSpec as P

EPSILON = 1e-05
MASKED = -1000000000.0


def in_order(parts, dim):
    parts = jnp.moveaxis(parts, 0, dim)
    lengths = parts.shape
    return parts.reshape(*lengths[:dim], lengths[dim] * lengths[dim + 1], *lengths[dim + 2 :])


def from_everyone(value, axis):
    count = lax.axis_size(axis)
    return lax.all_to_all(
        jnp.broadcast_to(value[None], (count, *value.shape)), axis, 0, 0, tiled=True
    )


def gather_directly(value, axis, dim):
    return in_order(from_everyone(value, axis), dim)


def picked(value, axis, root):
    return lax.dynamic_index_in_dim(lax.all_gather(value, axis), root, 0, keepdims=False)


def of_everyone(value, axis):
    everything = from_everyone(value, axis)
    return jnp.max(everything, axis=0)


def over_copies(value, axis):
    return from_everyone(value, axis).sum(axis=0)


def standardize_features(field):
    field = field.astype(jnp.float32)
    center = field - jnp.mean(field, axis=-1, keepdims=True)
    spread = jnp.mean(center * center, axis=-1, keepdims=True)
    return center * lax.rsqrt(spread + EPSILON)


def local(
    homolog_matrix,
    contact_matrix,
    genuine_homolog_total,
    genuine_chain_length,
    tensor_product_matrices,
    tensor_product_final,
    mixing_value_gate_matrix,
    mixing_logit_matrix,
    mixing_final_matrix,
    feedforward_gate_expand,
    feedforward_shrink_matrix,
):
    homolog_rows_local, chain_positions_local, homolog_rows_full = homolog_matrix.shape
    rows_dev = contact_matrix.shape[0]
    pair_width = contact_matrix.shape[2]
    outer_width = tensor_product_matrices.shape[2] // 2
    head_count = mixing_logit_matrix.shape[2]
    hidden_width = mixing_final_matrix.shape[1]
    head_width = hidden_width // head_count
    trans_width = feedforward_shrink_matrix.shape[1]
    row_blocks = rows_dev // 8
    row_index = lax.axis_index("row")
    col_index = lax.axis_index("col")
    ratio = lax.axis_size("row") // lax.axis_size("col")
    total_seqs = homolog_rows_local * lax.axis_size("row")
    seq_ids = row_index * homolog_rows_local + jnp.arange(homolog_rows_local, dtype=jnp.int32)
    res_ids = col_index * chain_positions_local + jnp.arange(chain_positions_local, dtype=jnp.int32)
    pair_ids = row_index * rows_dev + jnp.arange(rows_dev, dtype=jnp.int32)
    seq_float = (seq_ids < genuine_homolog_total[0]).astype(jnp.float32)
    res_valid = res_ids < genuine_chain_length[0]
    res_float = res_valid.astype(jnp.float32)
    row_float = (pair_ids < genuine_chain_length[0]).astype(jnp.float32)
    divisor = jnp.maximum(
        genuine_homolog_total[0].astype(jnp.float32) * row_float[:, None] * res_float[None, :], 1.0
    )
    starts = jnp.arange(row_blocks, dtype=jnp.int32) * 8
    standardized_source = standardize_features(homolog_matrix).astype(jnp.bfloat16)
    reshaped_tensor = standardized_source.reshape(
        homolog_rows_local * chain_positions_local, homolog_rows_full
    )
    projected = jnp.dot(
        reshaped_tensor, tensor_product_matrices[0], preferred_element_type=jnp.float32
    ).reshape(homolog_rows_local, chain_positions_local, 2 * outer_width)
    projected = (projected * (seq_float[:, None, None] * res_float[None, :, None])).astype(
        jnp.bfloat16
    )
    packed = projected.reshape(homolog_rows_local, chain_positions_local * 2 * outer_width)
    columns = gather_directly(packed, "row", 0).reshape(
        total_seqs, chain_positions_local, 2 * outer_width
    )
    left_all = columns[:, :, :outer_width].reshape(total_seqs, chain_positions_local * outer_width)
    right = columns[:, :, outer_width:].reshape(total_seqs, chain_positions_local * outer_width)
    left_cols = picked(left_all, "col", row_index // ratio).reshape(
        total_seqs, chain_positions_local, outer_width
    )
    outer_weight = tensor_product_final[0]

    def outer_rows(inputs):
        start, pair_rows = inputs
        rows = lax.dynamic_slice_in_dim(left_cols, start, 8, 1).reshape(total_seqs, 8 * outer_width)
        product = lax.dot_general(
            rows, right, (((0,), (0,)), ((), ())), preferred_element_type=jnp.float32
        )
        product = product.reshape(8, outer_width, chain_positions_local, outer_width).transpose(
            0, 2, 1, 3
        )
        product = product.reshape(8, chain_positions_local, outer_width * outer_width)
        scale = lax.dynamic_slice_in_dim(divisor, start, 8, 0)
        outer = (product / scale[:, :, None]).astype(jnp.bfloat16)
        update = jnp.dot(
            outer.reshape(8 * chain_positions_local, outer_width * outer_width),
            outer_weight,
            preferred_element_type=jnp.float32,
        )
        return (
            pair_rows.astype(jnp.float32) + update.reshape(8, chain_positions_local, pair_width)
        ).astype(jnp.bfloat16)

    contact_matrix = lax.map(
        outer_rows,
        (starts, contact_matrix.reshape(row_blocks, 8, chain_positions_local, pair_width)),
    ).reshape(rows_dev, chain_positions_local, pair_width)
    bias_weight = mixing_logit_matrix[0]

    def norm_rows(pair_rows):
        normed_rows = standardize_features(pair_rows).astype(jnp.bfloat16)
        logit_rows = jnp.dot(
            normed_rows.reshape(8 * chain_positions_local, pair_width),
            bias_weight,
            preferred_element_type=jnp.float32,
        )
        return (normed_rows, logit_rows.reshape(8, chain_positions_local, head_count))

    pair_normed, logits = lax.map(
        norm_rows, contact_matrix.reshape(row_blocks, 8, chain_positions_local, pair_width)
    )
    logits = jnp.where(
        res_valid[None, :, None],
        logits.reshape(rows_dev, chain_positions_local, head_count),
        MASKED,
    )
    logits = logits.transpose(0, 2, 1)
    peak = of_everyone(jnp.max(logits, axis=2), "col")
    expo = jnp.exp(logits - peak[:, :, None])
    totals = over_copies(jnp.sum(expo, axis=2), "col")
    local_weights = (expo / totals[:, :, None]).astype(jnp.bfloat16)
    part_rows = rows_dev // lax.axis_size("row")
    sectioned = local_weights.reshape(1, rows_dev, head_count, 1, chain_positions_local)
    moved = lax.all_to_all(
        lax.all_to_all(sectioned, "row", split_axis=1, concat_axis=0, tiled=True),
        "col",
        split_axis=0,
        concat_axis=3,
        tiled=True,
    )
    moved = moved.reshape(
        ratio, part_rows, head_count, lax.axis_size("col") * chain_positions_local
    )
    mine = gather_directly(moved, "row", 1).reshape(
        chain_positions_local, head_count, lax.axis_size("col") * chain_positions_local
    )
    value_weight = mixing_value_gate_matrix[0][:, :hidden_width]
    gate_weight = mixing_value_gate_matrix[0][:, hidden_width:]
    gate = jax.nn.sigmoid(
        jnp.dot(reshaped_tensor, gate_weight, preferred_element_type=jnp.float32)
    ).reshape(homolog_rows_local, chain_positions_local, hidden_width)
    values_local = jnp.dot(reshaped_tensor, value_weight, preferred_element_type=jnp.float32)
    values_local = values_local.astype(jnp.bfloat16).reshape(
        homolog_rows_local, chain_positions_local, hidden_width
    )
    values_piece = lax.all_gather(values_local, "col", axis=1, tiled=True)
    count = values_piece.shape[1]
    heads_piece = values_piece.reshape(homolog_rows_local, count, head_count, head_width)
    averaged = jnp.einsum("ihj,sjhc->sihc", mine, heads_piece, preferred_element_type=jnp.float32)
    gated = (
        gate * averaged.reshape(homolog_rows_local, chain_positions_local, hidden_width)
    ).astype(jnp.bfloat16)
    contact_increment = jnp.dot(
        gated.reshape(homolog_rows_local * chain_positions_local, hidden_width),
        mixing_final_matrix[0],
        preferred_element_type=jnp.float32,
    )
    homolog_matrix = (
        homolog_matrix.astype(jnp.float32)
        + contact_increment.reshape(homolog_rows_local, chain_positions_local, homolog_rows_full)
    ).astype(jnp.bfloat16)
    up_weight = feedforward_gate_expand[0]
    down_weight = feedforward_shrink_matrix[0]

    def transition_rows(inputs):
        pair_rows, normed_rows = inputs
        hidden = jnp.dot(
            normed_rows.reshape(8 * chain_positions_local, pair_width),
            up_weight,
            preferred_element_type=jnp.float32,
        )
        active = (jax.nn.silu(hidden[:, :trans_width]) * hidden[:, trans_width:]).astype(
            jnp.bfloat16
        )
        update = jnp.dot(active, down_weight, preferred_element_type=jnp.float32)
        return (
            pair_rows.astype(jnp.float32) + update.reshape(8, chain_positions_local, pair_width)
        ).astype(jnp.bfloat16)

    contact_matrix = lax.map(
        transition_rows,
        (contact_matrix.reshape(row_blocks, 8, chain_positions_local, pair_width), pair_normed),
    )
    contact_matrix = contact_matrix.reshape(rows_dev, chain_positions_local, pair_width)
    return (homolog_matrix, contact_matrix)


def solution(mesh):
    in_specs = (
        P("row", "col", None),
        P("row", "col", None),
        P(),
        P(),
        P(),
        P(),
        P(),
        P(),
        P(),
        P(),
        P(),
    )
    out_specs = (P("row", "col", None), P("row", "col", None))
    return jax.shard_map(local, mesh=mesh, in_specs=in_specs, out_specs=out_specs, check_vma=False)
```

profile of v0, /device:TPU:1, one launch (start us, length us, event | category | flops | bytes accessed | tf_op | source)
XLA Modules:
  0.0 399.5 jit_solution(8511673040539516351)
XLA Ops:
  12.9 40.4 %all_to_all.47 = bf16[16,8,5120]{2,1,0:T(8,128)(2,1)} all-to-all(bf16[16,8,5120]{2,1,0:T(8,128)(2,1)S(1)} %broadcast_in_dim.40), channel_id=1, replica_groups=mesh['row'=16,'col'=16] {'row'}, dimensions={0} | all-to-all | bytes 2621440 | tf_op jit(solution)/shard_map/all_to_all | solution.py:18
  53.3 3.3 reshape_reshape.3
  56.7 3.2 fusion.53
  59.9 4.4 %copy.88 = bf16[128,80,32]{0,2,1:T(8,128)(2,1)S(1)} copy(bf16[128,80,32]{2,1,0:T(8,128)(2,1)} %get-tuple-element.149) | data formatting | bytes 1310720 | tf_op jit(solution)/shard_map/slice | solution.py:98
  67.2 3.6 copy.91
  70.9 119.9 %all-gather.5.cloned.1.call-done = bf16[16,128,2560]{2,1,0:T(8,128)(2,1)} async-done(((bf16[1,128,2560]{2,1,0:T(8,128)(2,1)}), bf16[16,128,2560]{2,1,0:T(8,128)(2,1)}) %all-gather.5.cloned.1.call-update) | async-done | bytes 10485776 | tf_op jit(solution)/shard_map/all_gather | solution.py:28
  192.8 77.5 %while.32 = (s32[]{:T(128)}, bf16[10,8,80,128]{3,2,1,0:T(8,128)(2,1)S(1)}, bf16[10,8,80,128]{3,2,1,0:T(8,128)(2,1)}, s32[10]{0:T(128)S(1)}, bf16[128,80,32]{0,2,...) while((s32[]{:T(128)}, ...), condition=%wide.region_3.4_spmd, body=%wide.region_2.3_spmd.sunk | while | flops 337100800 | bytes 15212199 | solution.py:126
  196.1 2.4 copy.125
  203.8 2.4 copy.125
  211.6 2.4 copy.125
  219.3 2.4 copy.125
  227.1 2.4 copy.125
  234.8 2.4 copy.125
  242.6 2.4 copy.125
  271.8 17.8 %while.33 = (s32[]{:T(128)}, bf16[10,8,80,128]{3,2,1,0:T(8,128)(2,1)}, f32[10,8,80,8]{2,3,1,0:T(8,128)S(1)}, bf16[10,8,80,128]{3,2,1,0:T(8,128)(2,1)S(1)}, bf16[128,8]{0,1:T(8,128)(2,1)S(1)}, /*index=5*/s32[]{:T(128)}) while((s32[]{:T(128)}, bf16[10,8,80,128]{3,2,1,0:T(8,128)(2,1)}, f32[10,8,80,8]{2,3,1,0:T(8,128)S(1)}, ...), condition=%wide.region_7.8_spmd, body=%wide.region_4.7_spmd.sunk | while | flops 2458242 | bytes 886861 | solution.py:141
  289.8 12.6 %all_to_all.48 = f32[16,80,8]{1,2,0:T(8,128)S(1)} all-to-all(f32[16,80,8]{1,2,0:T(8,128)S(1)} %broadcast_in_dim.66), channel_id=1, replica_groups=mesh['row'=16,'col'=16] {'col'}, dimensions={0} | all-to-all | bytes 81920 | tf_op jit(solution)/shard_map/all_to_all | solution.py:18
  302.9 12.6 %all_to_all.49 = f32[16,80,8]{1,2,0:T(8,128)S(1)} all-to-all(f32[16,80,8]{1,2,0:T(8,128)S(1)} %broadcast_in_dim.67), channel_id=1, replica_groups=mesh['row'=16,'col'=16] {'col'}, dimensions={0} | all-to-all | bytes 81920 | tf_op jit(solution)/shard_map/all_to_all | solution.py:18
  315.9 14.2 %all_to_all.50 = bf16[1,80,8,1,80]{4,2,3,0,1:T(8,128)(2,1)} all-to-all(bf16[1,80,8,1,80]{4,2,3,0,1:T(8,128)(2,1)S(1)} %fusion.47), channel_id=1, replica_groups=mesh['row'=16,'col'=16] {'row'}, dimensions={1} | all-to-all | bytes 204800 | tf_op jit(solution)/shard_map/all_to_all | solution.py:157
  330.1 5.3 %all-to-all-start.4 = ((bf16[16,5,8,1,80]{4,2,1,3,0:T(8,128)(2,1)}), bf16[16,5,8,1,80]{4,2,1,3,0:T(8,128)(2,1)S(1)}, u32[]{:S(2)}, u32[]{:S(2)}) async-start(bf16[16,5,8,1,80]{4,2,1,3,0:T(8,128)(2,1)} %bitcast.37), calls=%async_computation.4 | async-start | bytes 327680 | tf_op jit(solution)/shard_map/all_to_all | solution.py:156
  335.4 8.6 %copy.85 = bf16[8,1280,256]{1,2,0:T(8,128)(2,1)} copy(bf16[8,1280,256]{2,0,1:T(8,128)(2,1)} %all-gather.3.cloned.1.call-done) | data formatting | bytes 10485760 | tf_op jit(solution)/shard_map/all_gather | solution.py:178
  347.3 4.4 %all-to-all-start.5 = ((bf16[16,1,5,8,1280]{4,3,2,1,0:T(8,128)(2,1)}), bf16[16,1,5,8,1280]{4,3,2,1,0:T(8,128)(2,1)}, u32[]{:S(2)}, u32[]{:S(2)}) async-start(bf16[16,1,5,8,1280]{4,3,2,1,0:T(8,128)(2,1)} %broadcast_in_dim.69), calls=%async_computation.5 | async-start | bytes 3276800 | tf_op jit(solution)/shard_map/all_to_all | solution.py:18
  353.2 26.3 %while.34 = (s32[]{:T(128)}, bf16[10,8,80,128]{3,2,1,0:T(8,128)(2,1)}, bf16[10,8,80,128]{3,2,1,0:T(8,128)(2,1)S(1)}, bf16[10,8,80,128]{3,2,1,0:T(8,128)(2,1)}, b...) while((s32[]{:T(128)}, bf16[10,8,80,128]{3,2,1,0:T(8,128)(2,1)}, ...), condition=%wide.region_13.14_spmd, body=%wide.region_12.13_spmd.sunk | while | flops 253870080 | bytes 7111249 | solution.py:212
  379.5 5.7 %all-to-all-done.5 = bf16[16,1,5,8,1280]{4,3,2,1,0:T(8,128)(2,1)} async-done(((bf16[16,1,5,8,1280]{4,3,2,1,0:T(8,128)(2,1)}), bf16[16,1,5,8,1280]{4,3,2,1,0:T(8,128)(2,1)}, u32[]{:S(2)}, u32[]{:S(2)}) %all-to-all-start.5) | async-done | bytes 1638432 | tf_op jit(solution)/shard_map/all_to_all | solution.py:18
  385.2 4.5 %fusion.29 = f32[8,80,8,32]{1,3,0,2:T(8,128)S(1)} fusion(bf16[80,8,1280,1]{2,1,0,3:T(8,128)(2,1)} %bitcast.41, bf16[8,1280,8,32]{1,3,2,0:T(8,128)(2,1)} %bitcast.170), kind=kOutput, calls=%fused_computation.40 | convolution fusion | flops 419430400 | bytes 7536640 | tf_op jit(solution)/shard_map/ihj,sjhc->sihc/dot_general | solution.py:181
  (222 shorter events, 104.1 us)
Async XLA Ops:
  7.2 384.1 %copy-start = (bf16[1,256,64]{1,2,0:T(8,128)(2,1)S(1)}, bf16[1,256,64]{1,2,0:T(8,128)(2,1)}, u32[]{:S(2)}) copy-start(bf16[1,256,64]{1,2,0:T(8,128)(2,1)} %param.25) | copy-start | bytes 98308
  7.2 183.5 %all-gather.5.cloned.1.call-start = ((), (), s32[]{:S(2)}) async-start(), calls=%async_computation.7 | async-start | bytes 11141120 | tf_op jit(solution)/shard_map/all_gather | solution.py:28
  64.3 1.4 copy-start.6
  65.4 1.9 copy-start.1
  65.4 270.0 %all-gather.3.cloned.1.call-start = ((), (), s32[]{:S(2)}) async-start(), calls=%async_computation.6 | async-start | bytes 5570560 | tf_op jit(solution)/shard_map/all_gather | solution.py:178
  191.9 1.0 copy-start.2
  270.3 1.5 copy-start.4
  270.4 1.5 copy-start.8
  330.1 15.7 %all-to-all-start.4 = ((bf16[16,5,8,1,80]{4,2,1,3,0:T(8,128)(2,1)}), bf16[16,5,8,1,80]{4,2,1,3,0:T(8,128)(2,1)S(1)}, u32[]{:S(2)}, u32[]{:S(2)}) async-start(bf16[16,5,8,1,80]{4,2,1,3,0:T(8,128)(2,1)} %bitcast.37), calls=%async_computation.4 | async-start | bytes 327680 | tf_op jit(solution)/shard_map/all_to_all | solution.py:156
  347.3 37.9 %all-to-all-start.5 = ((bf16[16,1,5,8,1280]{4,3,2,1,0:T(8,128)(2,1)}), bf16[16,1,5,8,1280]{4,3,2,1,0:T(8,128)(2,1)}, u32[]{:S(2)}, u32[]{:S(2)}) async-start(bf16[16,1,5,8,1280]{4,3,2,1,0:T(8,128)(2,1)} %broadcast_in_dim.69), calls=%async_computation.5 | async-start | bytes 3276800 | tf_op jit(solution)/shard_map/all_to_all | solution.py:18
  351.7 1.4 copy-start.3
  351.7 1.4 copy-start.7
  390.9 0.9 copy-start.5
Sparse Core Ops, SparseCore 0:
  65.5 125.1 all-gather.4
  193.4 79.3 all-gather.2
where the time goes:
time: 405 us; the launch traced here: 400 us
  waiting for transfers between devices  127 us (31%)
  blocking collectives  79.9 us (20%)
  local copies, waits for them, and re-layouts  73.5 us (18%)
  matrix products  44.7 us (11%)
  other arithmetic  28.4 us (7%)
  loops' own time  20.3 us (5%)
  between operations  15.7 us (4%)
  starting transfers between devices  9.78 us (2%)
    all_gather x1, waiting for transfers between devices, picked(): lax.all_gather(value, axis)  120 us
    all_to_all x3, blocking collectives, from_everyone(): lax.all_to_all(jnp.broadcast_to(value[None], (count, *value.shape)), axis...  65.7 us
    transpose x10, local copies, waits for them, and re-layouts, outer_rows(): product.reshape(8, outer_width, chain_positions_local, outer_width)  23.8 us
    another operation x1, loops' own time, local(): lax.map(outer_rows, (starts, contact_matrix.reshape(row_blocks, 8, chain_...  19.9 us
    dot_general x10, matrix products, outer_rows(): jnp.dot(outer.reshape(8 * chain_positions_local, outer_width * outer_widt...  17.1 us
    dynamic_update_slice x20, other arithmetic, local(): lax.map(outer_rows, (starts, contact_matrix.reshape(row_blocks, 8, chain_...  16.3 us
    dynamic_slice x20, local copies, waits for them, and re-layouts, local(): lax.map(outer_rows, (starts, contact_matrix.reshape(row_blocks, 8, chain_...  15.1 us
    all_to_all x1, blocking collectives, local(): lax.all_to_all(sectioned, 'row', split_axis=1, concat_axis=0, tiled=True)  14.2 us
  transfers between devices with their start and end apart: 4, of which 3 were waited for; matrix products, arithmetic and copies ran while one was open for 30% of the time, Pallas kernels for 0%

commit v1 on v0

v1 whole, which is shorter than its diff:
```python
import jax
import jax.numpy as jnp
from jax import lax
from jax.experimental import pallas as pl
from jax.experimental.pallas import tpu as pltpu

F32 = jnp.float32
BF = jnp.bfloat16


def normalize(field):
    center = field - jnp.mean(field, axis=-1, keepdims=True)
    spread = jnp.mean(center * center, axis=-1, keepdims=True)
    return center * lax.rsqrt(spread + 1e-5)


def full(shape):
    return pl.BlockSpec(shape, lambda *_: (0,) * len(shape))


def prologue_body(scal, homolog, left_weight, right_weight, normed_out, left_out, right_out, left_rows, right_rows):
    normed = normalize(homolog[...].astype(F32)).astype(BF)
    normed_out[...] = jnp.concatenate([normed[s] for s in range(8)], axis=1)
    projected = jnp.dot(normed.reshape(640, 64), left_weight[...], preferred_element_type=F32)
    left_rows[...] = projected.reshape(8, 80, 128)
    lane = lax.broadcasted_iota(jnp.int32, (8, 128), 1)
    seq_ok = scal[2] + lax.broadcasted_iota(jnp.int32, (8, 128), 0) < scal[0]
    group = lane // 32
    for q in range(20):
        piece = left_rows[:, 4 * q, :]
        for k in range(1, 4):
            piece = jnp.where(group == k, left_rows[:, 4 * q + k, :], piece)
        ok = seq_ok & (scal[3] + 4 * q + group < scal[1])
        left_out[:, q * 128 : (q + 1) * 128] = jnp.where(ok, piece, 0.0).astype(BF)
    for s in range(8):
        rows = jnp.concatenate([normed[s], jnp.zeros((48, 64), BF)], axis=0)
        right_rows[s] = lax.dot_general(
            right_weight[...], rows, (((1,), (1,)), ((), ())), preferred_element_type=F32
        )
    ok = seq_ok & (scal[3] + lane < scal[1])
    pieces = [jnp.where(ok, right_rows[:, d, :], 0.0)[:, :80] for d in range(32)]
    right_out[...] = jnp.concatenate(pieces, axis=1).astype(BF)


def prologue(scal, homolog, left_weight, right_weight):
    return pl.pallas_call(
        prologue_body,
        grid_spec=pltpu.PrefetchScalarGridSpec(
            num_scalar_prefetch=1,
            grid=(1,),
            in_specs=[full((8, 80, 64)), full((64, 128)), full((32, 64))],
            out_specs=[full((80, 512)), full((8, 2560)), full((8, 2560))],
            scratch_shapes=[pltpu.VMEM((8, 80, 128), F32), pltpu.VMEM((8, 32, 128), F32)],
        ),
        out_shape=[
            jax.ShapeDtypeStruct((80, 512), BF),
            jax.ShapeDtypeStruct((8, 2560), BF),
            jax.ShapeDtypeStruct((8, 2560), BF),
        ],
        name="prologue",
    )(scal, homolog, left_weight, right_weight)


def transition_body(contact, up_weight, down_weight, out):
    rows = contact[...].astype(F32)
    normed = normalize(rows).astype(BF)
    hidden = jnp.dot(normed, up_weight[...], preferred_element_type=F32)
    gate = hidden[:, :512]
    active = (gate * jax.nn.sigmoid(gate) * hidden[:, 512:]).astype(BF)
    out[...] = (rows + jnp.dot(active, down_weight[...], preferred_element_type=F32)).astype(BF)


def transition(contact, up_weight, down_weight):
    return pl.pallas_call(
        transition_body,
        grid=(10,),
        in_specs=[pl.BlockSpec((640, 128), lambda g: (g, 0)), full((128, 1024)), full((512, 128))],
        out_specs=pl.BlockSpec((640, 128), lambda g: (g, 0)),
        out_shape=jax.ShapeDtypeStruct((6400, 128), BF),
        compiler_params=pltpu.CompilerParams(vmem_limit_bytes=32 * 1024 * 1024),
        cost_estimate=pl.CostEstimate(flops=6400 * 128 * 1024 * 3, bytes_accessed=3300000, transcendentals=6400 * 512),
        name="transition",
    )(contact, up_weight, down_weight)


def average_body(weights, everyone, normed, homolog, value_weight, gate_weight, final_weight, out, scaled):
    def stat(a, k):
        return jnp.sum(weights[a, 80:96, :].astype(F32)[k : k + 3], axis=0, keepdims=True)

    peaks = [stat(a, 0) for a in range(16)]
    peak = peaks[0]
    for a in range(1, 16):
        peak = jnp.maximum(peak, peaks[a])
    factors = [jnp.exp(p - peak) for p in peaks]
    total = factors[0] * stat(0, 3)
    for a in range(1, 16):
        total = total + factors[a] * stat(a, 3)
    for a in range(16):
        scaled[a * 80 : (a + 1) * 80, :] = (weights[a, :80, :].astype(F32) * (factors[a] / total)).astype(BF)
    mixed = lax.dot_general(
        scaled[...], everyone[...], (((0,), (0,)), ((), ())), preferred_element_type=F32
    ).astype(BF)
    own = normed[...]
    sums = [None, None]
    for h in range(8):
        for q in range(2):
            value = jnp.dot(mixed[h * 80 : (h + 1) * 80, q * 256 : (q + 1) * 256], value_weight[h], preferred_element_type=F32)
            gate = jnp.dot(own[:, q * 256 : (q + 1) * 256], gate_weight[h], preferred_element_type=F32)
            gated = (jax.nn.sigmoid(gate) * value).astype(BF)
            term = jnp.dot(gated, final_weight[h], preferred_element_type=F32)
            sums[q] = term if sums[q] is None else sums[q] + term
    for s in range(8):
        out[s] = (homolog[s].astype(F32) + sums[s // 4][:, (s % 4) * 64 : (s % 4 + 1) * 64]).astype(BF)


def average(weights, everyone, normed, homolog, value_weight, gate_weight, final_weight):
    return pl.pallas_call(
        average_body,
        grid=(1,),
        in_specs=[
            full((16, 96, 640)), full((1280, 512)), full((80, 512)), full((8, 80, 64)),
            full((8, 256, 128)), full((8, 256, 128)), full((8, 128, 256)),
        ],
        out_specs=full((8, 80, 64)),
        out_shape=jax.ShapeDtypeStruct((8, 80, 64), BF),
        scratch_shapes=[pltpu.VMEM((1280, 640), BF)],
        compiler_params=pltpu.CompilerParams(vmem_limit_bytes=48 * 1024 * 1024),
        name="average",
    )(weights, everyone, normed, homolog, value_weight, gate_weight, final_weight)


ROWS = 8


def outer_body(scal, left, right, contact, final_weight, logit_weight, contact_out, weights_out, left_t, right_p, products, expo):
    step = pl.program_id(0)

    @pl.when(step == 0)
    def _():
        left_t[...] = jnp.transpose(left[...].astype(F32).reshape(128, 2560)).astype(BF)
        rows = right[...].astype(F32).reshape(128, 2560)
        for d in range(32):
            right_p[:, d * 128 : d * 128 + 80] = rows[:, d * 80 : (d + 1) * 80].astype(BF)
            right_p[:, d * 128 + 80 : (d + 1) * 128] = jnp.zeros((128, 48), BF)

    inverse = 1.0 / scal[0].astype(F32)
    lane = lax.broadcasted_iota(jnp.int32, (8, 128), 1)
    real = scal[3] + lane < scal[1]
    rows = left_t[pl.ds(pl.multiple_of(step * 256, 256), 256), :]
    for n in range(8):
        product = jnp.dot(rows, right_p[:, n * 512 : (n + 1) * 512], preferred_element_type=F32)
        product = (product * inverse).astype(BF)
        for i in range(ROWS):
            for q in range(4):
                d = n * 4 + q
                products[d * 32 : (d + 1) * 32, i * 128 : (i + 1) * 128] = product[
                    i * 32 : (i + 1) * 32, q * 128 : (q + 1) * 128
                ]
    for i in range(ROWS):
        if i % 2 == 0:
            update = jnp.dot(
                final_weight[...], products[:, i * 128 : (i + 2) * 128], preferred_element_type=F32
            )
        mine = jnp.transpose(update[:, (i % 2) * 128 : (i % 2 + 1) * 128])[:80]
        fresh = (contact[i].astype(F32) + mine).astype(BF)
        contact_out[i] = fresh
        normed = normalize(fresh.astype(F32)).astype(BF)
        normed = jnp.concatenate([normed, jnp.zeros((48, 128), BF)], axis=0)
        logits = lax.dot_general(
            logit_weight[...], normed, (((1,), (1,)), ((), ())), preferred_element_type=F32
        )
        logits = jnp.where(real, logits, -1e9)
        peak = jnp.max(jnp.where(lane < 80, logits, -3e38), axis=-1, keepdims=True)
        terms = jnp.where(lane < 80, jnp.exp(logits - peak), 0.0)
        total = jnp.sum(terms, axis=-1, keepdims=True)
        for k, value in enumerate((peak, total)):
            high = value.astype(BF).astype(F32)
            middle = (value - high).astype(BF).astype(F32)
            for t, part in enumerate((high, middle, value - high - middle)):
                terms = jnp.where(lane == 80 + 3 * k + t, part, terms)
        expo[:, pl.ds(step * ROWS + i, 1), :] = terms[:, None, :]

    @pl.when(step == 80 // ROWS - 1)
    def _():
        weights_out[...] = jnp.transpose(expo[...].reshape(640, 128))[:96].astype(BF)


def outer(scal, left, right, contact, final_weight, logit_weight):
    return pl.pallas_call(
        outer_body,
        grid_spec=pltpu.PrefetchScalarGridSpec(
            num_scalar_prefetch=1,
            grid=(80 // ROWS,),
            in_specs=[
                full((16, 8, 2560)), full((16, 8, 2560)),
                pl.BlockSpec((ROWS, 80, 128), lambda g, s: (g, 0, 0)),
                full((128, 1024)), full((8, 128)),
            ],
            out_specs=[pl.BlockSpec((ROWS, 80, 128), lambda g, s: (g, 0, 0)), full((96, 640))],
            scratch_shapes=[
                pltpu.VMEM((2560, 128), BF), pltpu.VMEM((128, 4096), BF),
                pltpu.VMEM((1024, 1024), BF), pltpu.VMEM((8, 80, 128), F32),
            ],
        ),
        out_shape=[jax.ShapeDtypeStruct((80, 80, 128), BF), jax.ShapeDtypeStruct((96, 640), BF)],
        compiler_params=pltpu.CompilerParams(vmem_limit_bytes=48 * 1024 * 1024),
        name="outer",
    )(scal, left, right, contact, final_weight, logit_weight)


def from_everyone(value, axis):
    return lax.all_to_all(
        jnp.broadcast_to(value[None], (lax.axis_size(axis), *value.shape)), axis, 0, 0, tiled=True
    )


def mirrored(value):
    size = lax.axis_size("row")
    pairs = [(r * size + c, c * size + r) for r in range(size) for c in range(size)]
    return lax.ppermute(value, ("row", "col"), pairs)


def spread(weight):
    heads, rows, columns = weight.shape
    eye = jnp.eye(4, dtype=weight.dtype)
    return (eye[None, :, None, :, None] * weight[:, None, :, None, :]).reshape(heads, 4 * rows, 4 * columns)


def local(
    homolog_matrix,
    contact_matrix,
    genuine_homolog_total,
    genuine_chain_length,
    tensor_product_matrices,
    tensor_product_final,
    mixing_value_gate_matrix,
    mixing_logit_matrix,
    mixing_final_matrix,
    feedforward_gate_expand,
    feedforward_shrink_matrix,
):
    row_index = lax.axis_index("row")
    col_index = lax.axis_index("col")
    scal = jnp.stack(
        [genuine_homolog_total[0], genuine_chain_length[0], row_index * 8, col_index * 80]
    ).astype(jnp.int32)
    left_weight = jnp.tile(tensor_product_matrices[0][:, :32], (1, 4))
    right_weight = tensor_product_matrices[0][:, 32:].T
    normed, left, right = prologue(scal, homolog_matrix, left_weight, right_weight)
    left = from_everyone(mirrored(left), "col")
    right = from_everyone(right, "row")
    everyone = lax.all_gather(normed, "col", tiled=True)
    final_weight = tensor_product_final[0].reshape(32, 32, 128).transpose(2, 1, 0).reshape(128, 1024)
    both = mixing_value_gate_matrix[0].reshape(64, 2, 8, 32).transpose(1, 2, 0, 3)
    value_weight = spread(both[0])
    gate_weight = spread(both[1])
    mixing_final = spread(mixing_final_matrix[0].reshape(8, 32, 64))
    contact, weights = outer(scal, left, right, contact_matrix, final_weight, mixing_logit_matrix[0].T)
    weights = from_everyone(mirrored(weights), "row")
    pair = transition(contact.reshape(6400, 128), feedforward_gate_expand[0], feedforward_shrink_matrix[0])
    msa = average(weights, everyone, normed, homolog_matrix, value_weight, gate_weight, mixing_final)
    return msa, pair.reshape(80, 80, 128)


def solution(mesh):
    split = jax.sharding.PartitionSpec("row", "col", None)
    whole = jax.sharding.PartitionSpec()
    return jax.shard_map(
        local, mesh=mesh, in_specs=(split, split) + (whole,) * 9, out_specs=(split, split), check_vma=False
    )
```

time: 405 us -> 218 us (0.54); the launches traced: 400 us -> 217 us
  blocking collectives: 79.9 us -> 0 us
  waiting for transfers between devices: 127 us -> 71.9 us
  local copies, waits for them, and re-layouts: 73.5 us -> 24.2 us
  Pallas kernels: 0 us -> 48.2 us
  starting transfers between devices: 9.78 us -> 55.4 us
  matrix products: 44.7 us -> 0 us
  other arithmetic: 28.4 us -> 2.14 us
  loops' own time: 20.3 us -> 0 us
    all_to_all x4 -> x0, blocking collectives: 79.9 us -> none  [the longest x3 65.7 us: from_everyone(): lax.all_to_all(jnp.broadcast_to(value[None], (count, *value.shape)), axis...]
    all_gather x2 -> x1, waiting for transfers between devices: 120 us -> 42.1 us  [local(): everyone = lax.all_gather(normed, 'col', tiled=True)]
    pallas_call x0 -> x4, Pallas kernels: none -> 48.2 us  [the longest x1 32 us: outer(): pl.pallas_call(outer_body, grid_spec=pltpu.PrefetchScalarGridSpec(num_sca...]
    dot_general x55 -> x0, matrix products: 44.7 us -> none  [the longest x10 17.1 us: outer_rows(): jnp.dot(outer.reshape(8 * chain_positions_local, outer_width * outer_widt...]
    all_to_all x2 -> x3, starting transfers between devices: 9.7 us -> 47.6 us  [from_everyone(): lax.all_to_all(jnp.broadcast_to(value[None], (lax.axis_size(axis), *value...]
    transpose x11 -> x2, local copies, waits for them, and re-layouts: 24.4 us -> 0.72 us  [the longest x1 0.61 us: local(): right_weight = tensor_product_matrices[0][:, 32:].T]
    another operation x3 -> x0, loops' own time: 20.3 us -> none  [the longest x1 19.9 us: local(): lax.map(outer_rows, (starts, contact_matrix.reshape(row_blocks, 8, chain_...]
    dynamic_slice x31 -> x0, local copies, waits for them, and re-layouts: 16.4 us -> none  [the longest x20 15.1 us: local(): lax.map(outer_rows, (starts, contact_matrix.reshape(row_blocks, 8, chain_...]
  transfers between devices with their start and end apart: 4 -> 6, of which waited for: 3 -> 5; matrix products, arithmetic and copies ran while one was open for 30% -> 5% of each run, Pallas kernels for 0% -> 5%
where the time goes in v1:
time: 218 us; the launch traced here: 217 us
  waiting for transfers between devices  71.9 us (33%)
  starting transfers between devices  55.4 us (25%)
  Pallas kernels  48.2 us (22%)
  local copies, waits for them, and re-layouts  24.2 us (11%)
  between operations  15.6 us (7%)
    all_to_all x3, starting transfers between devices, from_everyone(): lax.all_to_all(jnp.broadcast_to(value[None], (lax.axis_size(axis), *value...  47.6 us
    all_gather x1, waiting for transfers between devices, local(): everyone = lax.all_gather(normed, 'col', tiled=True)  42.1 us
    pallas_call x1, Pallas kernels, outer(): pl.pallas_call(outer_body, grid_spec=pltpu.PrefetchScalarGridSpec(num_sca...  32 us
    all_to_all x3, waiting for transfers between devices, from_everyone(): lax.all_to_all(jnp.broadcast_to(value[None], (lax.axis_size(axis), *value...  23.6 us
    pallas_call x1, Pallas kernels, transition(): pl.pallas_call(transition_body, grid=(10,), in_specs=[pl.BlockSpec((640,...  10.6 us
    unnamed x33, local copies, waits for them, and re-layouts  10.4 us
    mul x14, local copies, waits for them, and re-layouts, spread(): eye[None, :, None, :, None] * weight[:, None, :, None, :]  8.14 us
    ppermute x2, starting transfers between devices, mirrored(): return lax.ppermute(value, ('row', 'col'), pairs)  7.77 us
  transfers between devices with their start and end apart: 6, of which 5 were waited for; matrix products, arithmetic and copies ran while one was open for 5% of the time, Pallas kernels for 5%

profile of v1, /device:TPU:1, one launch (start us, length us, event | category | flops | bytes accessed | tf_op | source)
XLA Modules:
  0.0 217.5 jit_solution(1704272052962809321)
XLA Ops:
  8.5 1.7 copy.35.homolog
  12.9 2.9 %prologue.1 = (bf16[80,512]{1,0:T(8,128)(2,1)}, bf16[8,2560]{1,0:T(8,128)(2,1)}, bf16[8,2560]{1,0:T(8,128)(2,1)}) custom-call(s32[4]{0:T(128)} %pad_add_fusion.scal, bf16[8,80,64]{2,1,0:T(8,128)(2,1)} %copy.35.homolog, bf16[64,128]{1,0:T(8,128)(2,1)} %copy.36.left_weight, bf16[32,64]{1,0:T(8,128)(2,1)} %get-tuple-element.22.right_weight), custom_call_target="tpu_custom_call" | custom-call | tf_op jit(solution)/shard_map/prologue/pallas_call | solution.py:46
  15.9 1.7 broadcast_in_dim.7
  17.5 9.1 %all-to-all-start.1 = ((bf16[16,8,2560]{2,1,0:T(8,128)(2,1)}), bf16[16,8,2560]{2,1,0:T(8,128)(2,1)S(1)}, u32[]{:S(2)}, u32[]{:S(2)}) async-start(bf16[16,8,2560]{2,1,0:T(8,128)(2,1)} %broadcast_in_dim.7), calls=%async_computation.1 | async-start | bytes 1310720 | tf_op jit(solution)/shard_map/all_to_all | solution.py:212
  26.7 4.5 %collective-permute-start = (bf16[8,2560]{1,0:T(8,128)(2,1)S(1)}, bf16[8,2560]{1,0:T(8,128)(2,1)S(1)}, u32[]{:S(2)}, u32[]{:S(2)}) collective-permute-start(bf16[8,2560]{1,0:T(8,128)(2,1)S(1)} %copy-done.13), channel_id=1, source_target_pairs={{0,0},{1,16},{2,32},{3,48},{4,64},{5,80},{6,96},{7,112},{8,128},{9... | collective-permute-start | bytes 122888 | tf_op jit(solution)/shard_map/ppermute | solution.py:220
  31.3 2.7 %collective-permute-done = bf16[8,2560]{1,0:T(8,128)(2,1)S(1)} collective-permute-done((bf16[8,2560]{1,0:T(8,128)(2,1)S(1)}, bf16[8,2560]{1,0:T(8,128)(2,1)S(1)}, u32[]{:S(2)}, u32[]{:S(2)}) %collective-permute-start) | collective-permute-done | bytes 40992 | tf_op jit(solution)/shard_map/ppermute | solution.py:220
  33.9 8.7 %all-to-all-done.1.right = bf16[16,8,2560]{2,1,0:T(8,128)(2,1)S(1)} async-done(((bf16[16,8,2560]{2,1,0:T(8,128)(2,1)}), bf16[16,8,2560]{2,1,0:T(8,128)(2,1)S(1)}, u32[]{:S(2)}, u32[]{:S(2)}) %all-to-all-start.1) | async-done | bytes 655392 | tf_op jit(solution)/shard_map/all_to_all | solution.py:212
  43.4 12.8 %all-to-all-start = ((bf16[16,8,2560]{2,1,0:T(8,128)(2,1)}), bf16[16,8,2560]{2,1,0:T(8,128)(2,1)S(1)}, u32[]{:S(2)}, u32[]{:S(2)}) async-start(bf16[16,8,2560]{2,1,0:T(8,128)(2,1)} %broadcast_in_dim.6), calls=%async_computation | async-start | bytes 1310720 | tf_op jit(solution)/shard_map/all_to_all | solution.py:212
  56.5 14.9 %all-to-all-done.left = bf16[16,8,2560]{2,1,0:T(8,128)(2,1)S(1)} async-done(((bf16[16,8,2560]{2,1,0:T(8,128)(2,1)}), bf16[16,8,2560]{2,1,0:T(8,128)(2,1)S(1)}, u32[]{:S(2)}, u32[]{:S(2)}) %all-to-all-start) | async-done | bytes 655392 | tf_op jit(solution)/shard_map/all_to_all | solution.py:212
  71.5 32.0 %outer.1 = (bf16[80,80,128]{2,1,0:T(8,128)(2,1)S(1)}, bf16[96,640]{1,0:T(8,128)(2,1)S(1)}) custom-call(s32[4]{0:T(128)S(1)} %copy-done.5, bf16[16,8,2560]{2,1,0:T(8,128)(2,1)S(1)} %all-to-all-done.left, bf16[16,8,2560]{2,1,0:T(8,128)(2,1)S(1)} %all-to-all-done.1.right, bf16[80,80,128]{2,1,0:T(8,128)(2,1)S(1)} %copy-done, ...), custom_call_target="tpu_custom_call" | custom-call | tf_op jit(solution)/shard_map/outer/pallas_call | solution.py:189
  103.4 1.2 copy-done.7
  104.6 3.2 %collective-permute-start.1 = (bf16[96,640]{1,0:T(8,128)(2,1)S(1)}, bf16[96,640]{1,0:T(8,128)(2,1)S(1)}, u32[]{:S(2)}, u32[]{:S(2)}) collective-permute-start(bf16[96,640]{1,0:T(8,128)(2,1)S(1)} %get-tuple-element.9), channel_id=1, source_target_pairs={{0,0},{1,16},{2,32},{3,48},{4,64},{5,80},{6,96},{7,112},{8,128},{9... | collective-permute-start | bytes 368648 | tf_op jit(solution)/shard_map/ppermute | solution.py:220
  107.9 2.9 %collective-permute-done.1 = bf16[96,640]{1,0:T(8,128)(2,1)S(1)} collective-permute-done((bf16[96,640]{1,0:T(8,128)(2,1)S(1)}, bf16[96,640]{1,0:T(8,128)(2,1)S(1)}, u32[]{:S(2)}, u32[]{:S(2)}) %collective-permute-start.1) | collective-permute-done | bytes 122912 | tf_op jit(solution)/shard_map/ppermute | solution.py:220
  110.8 1.4 broadcast_in_dim.8
  112.2 25.7 %all-to-all-start.2 = ((bf16[16,96,640]{2,1,0:T(8,128)(2,1)}), bf16[16,96,640]{2,1,0:T(8,128)(2,1)S(1)}, u32[]{:S(2)}, u32[]{:S(2)}) async-start(bf16[16,96,640]{2,1,0:T(8,128)(2,1)} %broadcast_in_dim.8), calls=%async_computation.2 | async-start | bytes 3932160 | tf_op jit(solution)/shard_map/all_to_all | solution.py:212
  140.6 1.0 copy.42
  142.7 1.3 mul.78
  144.7 1.0 copy.41
  148.1 1.4 broadcast_multiply_fusion.1
  149.8 10.6 %transition.1 = bf16[6400,128]{1,0:T(8,128)(2,1)} custom-call(bf16[6400,128]{1,0:T(8,128)(2,1)S(1)} %bitcast.32, bf16[128,1024]{1,0:T(8,128)(2,1)S(1)} %bitcast.33, bf16[512,128]{1,0:T(8,128)(2,1)S(1)} %bitcast.34), custom_call_target="tpu_custom_call" | custom-call | flops 2516582400 | bytes 3300000 | tf_op jit(solution)/shard_map/transition/pallas_call | solution.py:74
  160.4 42.1 %all-gather.2.cloned.1.call-done.everyone = bf16[1280,512]{1,0:T(8,128)(2,1)} async-done(((bf16[80,512]{1,0:T(8,128)(2,1)}), bf16[1280,512]{1,0:T(8,128)(2,1)}) %all-gather.2.cloned.1.call-update) | async-done | bytes 1310736 | tf_op jit(solution)/shard_map/all_gather | solution.py:252
  203.4 1.3 copy-done.2
  205.6 2.7 %average.1 = bf16[8,80,64]{2,1,0:T(8,128)(2,1)S(1)} custom-call(bf16[16,96,640]{2,1,0:T(8,128)(2,1)S(1)} %all-to-all-done.2.weights, bf16[1280,512]{1,0:T(8,128)(2,1)S(1)} %copy-done.2, bf16[80,512]{1,0:T(8,128)(2,1)S(1)} %copy-done.4, bf16[8,80,64]{2,1,0:T(8,128)(2,1)S(1)} %copy-done.1, bf16[8,256,128]{2,1,0:T(8,128)(2,1)S(1)} %get-tuple-element.21.value_weight, ...), custom_call_target="tpu_custom_call" | custom-call | tf_op jit(solution)/shard_map/average/pallas_call | solution.py:117
  208.9 1.7 copy.46
  (53 shorter events, 13.4 us)
Async XLA Ops:
  15.9 10.9 %copy-start.13 = (bf16[8,2560]{1,0:T(8,128)(2,1)S(1)}, bf16[8,2560]{1,0:T(8,128)(2,1)}, u32[]{:S(2)}) copy-start(bf16[8,2560]{1,0:T(8,128)(2,1)} %get-tuple-element.7) | copy-start | bytes 122884
  17.5 38.7 %copy-start.11 = (bf16[1,1024,128]{2,1,0:T(8,128)(2,1)S(1)}, bf16[1,1024,128]{2,1,0:T(8,128)(2,1)}, u32[]{:S(2)}) copy-start(bf16[1,1024,128]{2,1,0:T(8,128)(2,1)} %param.16) | copy-start | bytes 786436
  17.5 25.0 %all-to-all-start.1 = ((bf16[16,8,2560]{2,1,0:T(8,128)(2,1)}), bf16[16,8,2560]{2,1,0:T(8,128)(2,1)S(1)}, u32[]{:S(2)}, u32[]{:S(2)}) async-start(bf16[16,8,2560]{2,1,0:T(8,128)(2,1)} %broadcast_in_dim.7), calls=%async_computation.1 | async-start | bytes 1310720 | tf_op jit(solution)/shard_map/all_to_all | solution.py:212
  26.7 44.8 %copy-start = (bf16[80,80,128]{2,1,0:T(8,128)(2,1)S(1)}, bf16[80,80,128]{2,1,0:T(8,128)(2,1)}, u32[]{:S(2)}) copy-start(bf16[80,80,128]{2,1,0:T(8,128)(2,1)} %contact.1) | copy-start | bytes 4915204
  26.7 44.8 %copy-start.5 = (s32[4]{0:T(128)S(1)}, s32[4]{0:T(128)}, u32[]{:S(2)}) copy-start(s32[4]{0:T(128)} %pad_add_fusion.scal) | copy-start | bytes 52
  26.7 44.8 %copy-start.6 = (bf16[1,128,8]{1,2,0:T(8,128)(2,1)S(1)}, bf16[1,128,8]{1,2,0:T(8,128)(2,1)}, u32[]{:S(2)}) copy-start(bf16[1,128,8]{1,2,0:T(8,128)(2,1)} %param.18) | copy-start | bytes 6148
  26.7 7.2 %collective-permute-start = (bf16[8,2560]{1,0:T(8,128)(2,1)S(1)}, bf16[8,2560]{1,0:T(8,128)(2,1)S(1)}, u32[]{:S(2)}, u32[]{:S(2)}) collective-permute-start(bf16[8,2560]{1,0:T(8,128)(2,1)S(1)} %copy-done.13), channel_id=1, source_target_pairs={{0,0},{1,16},{2,32},{3,48},{4,64},{5,80},{6,96},{7,112},{8,128},{9... | collective-permute-start | bytes 122888 | tf_op jit(solution)/shard_map/ppermute | solution.py:220
  43.4 28.0 %all-to-all-start = ((bf16[16,8,2560]{2,1,0:T(8,128)(2,1)}), bf16[16,8,2560]{2,1,0:T(8,128)(2,1)S(1)}, u32[]{:S(2)}, u32[]{:S(2)}) async-start(bf16[16,8,2560]{2,1,0:T(8,128)(2,1)} %broadcast_in_dim.6), calls=%async_computation | async-start | bytes 1310720 | tf_op jit(solution)/shard_map/all_to_all | solution.py:212
  103.4 1.2 copy-start.7
  104.6 6.2 %collective-permute-start.1 = (bf16[96,640]{1,0:T(8,128)(2,1)S(1)}, bf16[96,640]{1,0:T(8,128)(2,1)S(1)}, u32[]{:S(2)}, u32[]{:S(2)}) collective-permute-start(bf16[96,640]{1,0:T(8,128)(2,1)S(1)} %get-tuple-element.9), channel_id=1, source_target_pairs={{0,0},{1,16},{2,32},{3,48},{4,64},{5,80},{6,96},{7,112},{8,128},{9... | collective-permute-start | bytes 368648 | tf_op jit(solution)/shard_map/ppermute | solution.py:220
  112.2 26.4 %copy-start.12 = (bf16[1,64,512]{2,1,0:T(8,128)(2,1)S(1)}, bf16[1,64,512]{2,1,0:T(8,128)(2,1)}, u32[]{:S(2)}) copy-start(bf16[1,64,512]{2,1,0:T(8,128)(2,1)} %param.17) | copy-start | bytes 196612
  112.2 90.3 %all-to-all-start.2 = ((bf16[16,96,640]{2,1,0:T(8,128)(2,1)}), bf16[16,96,640]{2,1,0:T(8,128)(2,1)S(1)}, u32[]{:S(2)}, u32[]{:S(2)}) async-start(bf16[16,96,640]{2,1,0:T(8,128)(2,1)} %broadcast_in_dim.8), calls=%async_computation.2 | async-start | bytes 3932160 | tf_op jit(solution)/shard_map/all_to_all | solution.py:212
  137.9 64.6 %all-gather.2.cloned.1.call-start = ((), (), s32[]{:S(2)}) async-start(), calls=%async_computation.3 | async-start | bytes 1392640 | tf_op jit(solution)/shard_map/all_gather | solution.py:252
  148.0 1.8 copy-start.8
  148.0 1.8 copy-start.9
  148.0 1.8 copy-start.10
  202.5 0.9 copy-start.1
  203.4 1.3 copy-start.2
  204.7 0.9 copy-start.4
  208.3 0.7 copy-start.3
Sparse Core Ops, SparseCore 0:
  142.0 60.4 all-gather.1

commit v2 on v1

v2 whole, which is shorter than its diff:
```python
import jax
import jax.numpy as jnp
from jax import lax
from jax.experimental import pallas as pl
from jax.experimental.pallas import tpu as pltpu

F32 = jnp.float32
BF = jnp.bfloat16
ROWS = 16


def normalize(field, axis=-1):
    center = field - jnp.mean(field, axis=axis, keepdims=True)
    spread = jnp.mean(center * center, axis=axis, keepdims=True)
    return center * lax.rsqrt(spread + 1e-5)


def full(shape):
    return pl.BlockSpec(shape, lambda *_: (0,) * len(shape))


def wide(value, lanes):
    missing = jnp.zeros((*value.shape[:-1], lanes - value.shape[-1]), value.dtype)
    return jnp.concatenate([value, missing], axis=-1)


def tall(value, rows):
    missing = jnp.zeros((rows - value.shape[0], *value.shape[1:]), value.dtype)
    return jnp.concatenate([value, missing], axis=0)


def call(body, scalars, grid, in_specs, out_specs, out_shape, scratch, cost, limit=48):
    flops, moved, special = cost
    return pl.pallas_call(
        body,
        grid_spec=pltpu.PrefetchScalarGridSpec(
            num_scalar_prefetch=scalars, grid=grid, in_specs=in_specs, out_specs=out_specs, scratch_shapes=scratch
        ),
        out_shape=out_shape,
        compiler_params=pltpu.CompilerParams(vmem_limit_bytes=limit * 1024 * 1024),
        cost_estimate=pl.CostEstimate(flops=flops, bytes_accessed=moved, transcendentals=special),
        name=body.__name__,
    )


def shaped(dtype, *dims):
    return jax.ShapeDtypeStruct(dims, dtype)


def prologue_body(seqs, residues, homolog, weight, left_out, shared_out, left_rows, right_rows):
    row, col = lax.axis_index("row"), lax.axis_index("col")
    normed = normalize(homolog[...].astype(F32), 1)
    rounded = normed.astype(BF)
    weights = weight[...].astype(F32)
    left_weight = jnp.concatenate([weights[:, :32]] * 4, axis=1).astype(BF)
    right_weight = jnp.transpose(wide(weights, 128))[32:64].astype(BF)
    for s in range(8):
        right_rows[s] = wide(jnp.dot(right_weight, rounded[s], preferred_element_type=F32), 128)
    turned = jnp.transpose(wide(normed.reshape(512, 80), 128))[:80].astype(BF)
    for k in range(5):
        shared_out[:16, k * 512 : (k + 1) * 512] = turned[k * 16 : (k + 1) * 16]
    for s in range(8):
        left_rows[s] = jnp.dot(turned[:, s * 64 : (s + 1) * 64], left_weight, preferred_element_type=F32)
    lane = lax.broadcasted_iota(jnp.int32, (8, 128), 1)
    seq_ok = row * 8 + lax.broadcasted_iota(jnp.int32, (8, 128), 0) < seqs[0]
    group = lane // 32
    for q in range(20):
        piece = left_rows[:, 4 * q, :]
        for k in range(1, 4):
            piece = jnp.where(group == k, left_rows[:, 4 * q + k, :], piece)
        ok = seq_ok & (col * 80 + 4 * q + group < residues[0])
        left_out[:, q * 128 : (q + 1) * 128] = jnp.where(ok, piece, 0.0).astype(BF)
    ok = seq_ok & (col * 80 + lane < residues[0])
    pieces = [jnp.where(ok, right_rows[:, d, :], 0.0)[:, :80] for d in range(32)]
    shared_out[16:, :] = jnp.concatenate(pieces, axis=1).astype(BF)


def prologue(seqs, residues, homolog, weight):
    return call(
        prologue_body, 2, (1,),
        [full((8, 64, 80)), full((64, 64))],
        [full((8, 2560)), full((24, 2560))],
        [shaped(BF, 8, 2560), shaped(BF, 24, 2560)],
        [pltpu.VMEM((8, 80, 128), F32), pltpu.VMEM((8, 32, 128), F32)],
        (10**8, 4 * 10**5, 10**4),
    )(seqs, residues, homolog, weight)


def weights_body(product, value_gate, mixing, product_out, value_out, gate_out, mixing_out, rows):
    rows[...] = product[...].astype(F32).reshape(32, 32, 128)
    swapped = jnp.concatenate([rows[:, d, :] for d in range(32)], axis=0)
    product_out[...] = jnp.transpose(swapped).astype(BF)
    value_out[...] = jnp.zeros_like(value_out)
    gate_out[...] = jnp.zeros_like(gate_out)
    mixing_out[...] = jnp.zeros_like(mixing_out)
    both = value_gate[...]
    final = jnp.transpose(tall(mixing[...].astype(F32), 128))[:, :64].astype(BF)
    for h in range(8):
        for s in range(4):
            value_out[h, s * 64 : (s + 1) * 64, s * 32 : (s + 1) * 32] = both[:, h * 32 : (h + 1) * 32]
            gate_out[h, s * 64 : (s + 1) * 64, s * 32 : (s + 1) * 32] = both[:, 256 + h * 32 : 288 + h * 32]
            mixing_out[h, s * 32 : (s + 1) * 32, s * 64 : (s + 1) * 64] = final[h * 32 : (h + 1) * 32]


def arrange_weights(product, value_gate, mixing):
    return call(
        weights_body, 0, (1,),
        [full((1024, 128)), full((64, 512)), full((64, 256))],
        [full((128, 1024)), full((8, 256, 128)), full((8, 256, 128)), full((8, 128, 256))],
        [shaped(BF, 128, 1024), shaped(BF, 8, 256, 128), shaped(BF, 8, 256, 128), shaped(BF, 8, 128, 256)],
        [pltpu.VMEM((32, 32, 128), F32)],
        (10**6, 2 * 10**6, 0),
    )(product, value_gate, mixing)


def outer_body(seqs, residues, left_a, left_b, right_a, right_b, right_c, right_d, contact, final_weight, logit_weight,
               contact_out, weights_out, left_t, right_p, products, expo, flat):
    step = pl.program_id(0)
    row, col = lax.axis_index("row"), lax.axis_index("col")

    @pl.when(step == 0)
    def _():
        for w, half in enumerate((left_a, left_b)):
            for v in range(4):
                for u in range(2):
                    flat[(w * 8 + v * 2 + u) * 8 : (w * 8 + v * 2 + u + 1) * 8, :] = half[v, u].astype(F32)
        left_t[...] = jnp.transpose(flat[...]).astype(BF)
        for m, part in enumerate((right_a, right_b, right_c, right_d)):
            for v in range(4):
                z = ((row >> 2) - v) & 3
                x = (row - m) & 3
                place = ((col ^ x) & 1) * 8 + (((col >> 2) - z) & 3) * 2 + (((col >> 1) ^ (x >> 1)) & 1)
                flat[pl.ds(pl.multiple_of(place * 8, 8), 8), :] = part[v].astype(F32)
        rows = flat[...]
        for d in range(32):
            right_p[:, d * 128 : (d + 1) * 128] = wide(rows[:, d * 80 : (d + 1) * 80], 128).astype(BF)

    inverse = 1.0 / seqs[0].astype(F32)
    lane = lax.broadcasted_iota(jnp.int32, (8 * ROWS, 128), 1)
    rows = left_t[pl.ds(pl.multiple_of(step * 32 * ROWS, 32 * ROWS), 32 * ROWS), :]
    for n in range(8):
        product = jnp.dot(rows, right_p[:, n * 512 : (n + 1) * 512], preferred_element_type=F32)
        product = (product * inverse).astype(BF)
        for i in range(ROWS):
            for q in range(4):
                d = n * 4 + q
                products[d * 32 : (d + 1) * 32, i * 128 : (i + 1) * 128] = product[
                    i * 32 : (i + 1) * 32, q * 128 : (q + 1) * 128
                ]
    updates = []
    for i in range(0, ROWS, 2):
        update = jnp.dot(final_weight[...], products[:, i * 128 : (i + 2) * 128], preferred_element_type=F32)
        updates += [jnp.transpose(update[:, :128])[:80], jnp.transpose(update[:, 128:])[:80]]
    fresh = contact[...].reshape(ROWS * 80, 128).astype(F32) + jnp.concatenate(updates, axis=0)
    fresh = fresh.astype(BF)
    contact_out[...] = fresh.reshape(ROWS, 80, 128)
    normed = normalize(fresh.astype(F32)).astype(BF)
    logits = jnp.concatenate(
        [
            lax.dot_general(
                logit_weight[...], tall(normed[i * 80 : (i + 1) * 80], 128), (((1,), (1,)), ((), ())),
                preferred_element_type=F32,
            )
            for i in range(ROWS)
        ],
        axis=0,
    )
    logits = jnp.where(col * 80 + lane < residues[0], logits, -1e9)
    peak = jnp.max(jnp.where(lane < 80, logits, -3e38), axis=-1, keepdims=True)
    terms = jnp.where(lane < 80, jnp.exp(logits - peak), 0.0)
    total = jnp.sum(terms, axis=-1, keepdims=True)
    for k, value in enumerate((peak, total)):
        high = value.astype(BF).astype(F32)
        middle = (value - high).astype(BF).astype(F32)
        for t, part in enumerate((high, middle, value - high - middle)):
            terms = jnp.where(lane == 80 + 3 * k + t, part, terms)
    expo[pl.ds(step * ROWS, ROWS)] = terms.reshape(ROWS, 8, 128)

    @pl.when(step == 80 // ROWS - 1)
    def _():
        for q in range(4):
            weights_out[q] = expo[pl.ds((((col >> 2) + q) & 3) * 20, 20)].reshape(160, 128).astype(BF)


def outer(seqs, residues, left, right, contact, final_weight, logit_weight):
    block = pl.BlockSpec((ROWS, 80, 128), lambda g, *_: (g, 0, 0))
    return call(
        outer_body, 2, (80 // ROWS,),
        [full((4, 2, 8, 2560))] * 2 + [full((4, 8, 2560))] * 4 + [block, full((128, 1024)), full((8, 128))],
        [block, full((4, 160, 128))],
        [shaped(BF, 80, 80, 128), shaped(BF, 4, 160, 128)],
        [
            pltpu.VMEM((2560, 128), BF), pltpu.VMEM((128, 4096), BF), pltpu.VMEM((1024, 128 * ROWS), BF),
            pltpu.VMEM((80, 8, 128), F32), pltpu.VMEM((128, 2560), F32),
        ],
        (12 * 10**9, 6 * 10**6, 10**5),
    )(seqs, residues, *left, *right, contact, final_weight, logit_weight)


def transition_body(contact, up_weight, down_weight, out):
    rows = contact[...].reshape(640, 128).astype(F32)
    normed = normalize(rows).astype(BF)
    hidden = jnp.dot(normed, up_weight[...], preferred_element_type=F32)
    gate = hidden[:, :512]
    active = (gate * jax.nn.sigmoid(gate) * hidden[:, 512:]).astype(BF)
    rows = rows + jnp.dot(active, down_weight[...], preferred_element_type=F32)
    out[...] = rows.astype(BF).reshape(8, 80, 128)


def transition(contact, up_weight, down_weight):
    block = pl.BlockSpec((8, 80, 128), lambda g: (g, 0, 0))
    return call(
        transition_body, 0, (10,),
        [block, full((128, 1024)), full((512, 128))],
        block, shaped(BF, 80, 80, 128), [],
        (5 * 10**9, 33 * 10**5, 6400 * 512), 32,
    )(contact, up_weight, down_weight)


def average_body(part_a, part_b, part_c, part_d, everyone_a, everyone_b, value_weight, gate_weight, final_weight,
                 out_a, out_b, out_c, out_d, scaled, mixed, normed):
    row, col = lax.axis_index("row"), lax.axis_index("col")
    parts = (part_a, part_b, part_c, part_d)
    blocks = [(x, z) for x in range(4) for z in range(4)]
    lane = lax.broadcasted_iota(jnp.int32, (160, 128), 1)

    def stat(x, z, k):
        here = (lane >= 80 + 3 * k) & (lane < 83 + 3 * k)
        return jnp.sum(jnp.where(here, parts[x][z].astype(F32), 0.0), axis=-1, keepdims=True)

    peaks = [stat(x, z, 0) for x, z in blocks]
    peak = peaks[0]
    for other in peaks[1:]:
        peak = jnp.maximum(peak, other)
    factors = [jnp.exp(p - peak) for p in peaks]
    total = sum(f * stat(x, z, 1) for f, (x, z) in zip(factors, blocks))
    inverse = 1.0 / total
    for factor, (x, z) in zip(factors, blocks):
        far_z = ((row >> 2) - z) & 3
        far_x = (row - x) & 3
        place = ((col ^ far_x) & 1) * 8 + (((col >> 2) - far_z) & 3) * 2 + (((col >> 1) ^ (far_x >> 1)) & 1)
        scaled[place] = parts[x][z].astype(F32) * (factor * inverse)
    for w, everyone in enumerate((everyone_a, everyone_b)):
        for v in range(4):
            for u in range(2):
                for k in range(5):
                    start = (w * 8 + v * 2 + u) * 80 + k * 16
                    for z in range(4):
                        normed[start : start + 16, z * 512 : (z + 1) * 512] = everyone[v, u, z, :, k * 512 : (k + 1) * 512]
    sums = None
    for w in range(2):
        rows = jnp.concatenate([scaled[w * 8 + k][:, :80] for k in range(8)], axis=1).astype(BF)
        term = jnp.dot(rows, normed[w * 640 : (w + 1) * 640, :], preferred_element_type=F32)
        sums = term if sums is None else sums + term
    mixed[...] = sums.reshape(20, 8, 2048)
    pick = lax.broadcasted_iota(jnp.int32, (24, 80), 1) - ((row >> 2) & 3) * 20
    pick = (pick == lax.broadcasted_iota(jnp.int32, (24, 80), 0)) & (pick < 20)
    own = jnp.dot(pick.astype(F32).astype(BF), normed[:80, :], preferred_element_type=F32)

    def stacked(value):
        return jnp.concatenate([value[:, g * 256 : (g + 1) * 256] for g in range(8)], axis=0).astype(BF)

    own = stacked(own)
    result = None
    for h in range(8):
        value = jnp.dot(stacked(tall(mixed[:, h, :], 24)), value_weight[h], preferred_element_type=F32)
        gate = jnp.dot(own, gate_weight[h], preferred_element_type=F32)
        gated = (jax.nn.sigmoid(gate) * value).astype(BF)
        term = jnp.dot(gated, final_weight[h], preferred_element_type=F32)
        result = term if result is None else result + term
    for v, out in enumerate((out_a, out_b, out_c, out_d)):
        out[...] = result[v * 48 : (v + 1) * 48]


def average(parts, everyone, value_weight, gate_weight, final_weight):
    return call(
        average_body, 0, (1,),
        [full((4, 160, 128))] * 4 + [full((4, 2, 4, 16, 2560))] * 2 + [
            full((8, 256, 128)), full((8, 256, 128)), full((8, 128, 256))
        ],
        [full((48, 256))] * 4, [shaped(F32, 48, 256)] * 4,
        [pltpu.VMEM((16, 160, 128), F32), pltpu.VMEM((20, 8, 2048), F32), pltpu.VMEM((1280, 2048), BF)],
        (3 * 10**9, 8 * 10**6, 10**5),
    )(*parts, *everyone, value_weight, gate_weight, final_weight)


def epilogue_body(part_a, part_b, part_c, part_d, homolog, out, pieces):
    row = lax.axis_index("row")
    for v, part in enumerate((part_a, part_b, part_c, part_d)):
        pieces[v] = part[...]
    for half in range(2):
        rows = jnp.concatenate(
            [pieces[(q - (row >> 2)) & 3][half * 24 : half * 24 + 20] for q in range(4)], axis=0
        )
        turned = jnp.transpose(tall(rows, 128))
        for s in range(4):
            fresh = homolog[half * 4 + s].astype(F32) + turned[s * 64 : (s + 1) * 64, :80]
            out[half * 4 + s] = fresh.astype(BF)


def epilogue(parts, homolog):
    return call(
        epilogue_body, 0, (1,),
        [full((48, 256))] * 4 + [full((8, 64, 80))], full((8, 64, 80)), shaped(BF, 8, 64, 80),
        [pltpu.VMEM((4, 48, 256), F32)],
        (10**6, 4 * 10**5, 0),
    )(*parts, homolog)


def place(z, x, y, h, core):
    return (z * 4 + x) * 16 + y * 4 + h * 2 + core


def route(value, target):
    pairs = []
    for index in range(256):
        row, col = divmod(index, 16)
        z, x, y, h, core = row >> 2, row & 3, col >> 2, (col >> 1) & 1, col & 1
        pairs.append((index, place(*target(z, x, y, h, core))))
    return lax.ppermute(value, ("row", "col"), pairs)


def along_x(value, m):
    return route(value, lambda z, x, y, h, c: (z, (x + m) % 4, y, h, c))


def along_z(value, m):
    return route(value, lambda z, x, y, h, c: ((z + m) % 4, x, y, h, c))


def along_y(value, m):
    return route(value, lambda z, x, y, h, c: (z, x, (y + m) % 4, h, c))


def along_x(value, m):
    return route(value, lambda z, x, y, h, c: (z, (x + m) % 4, y, h, c))


def along_z(value, m):
    return route(value, lambda z, x, y, h, c: ((z + m) % 4, x, y, h, c))


def along_y(value, m):
    return route(value, lambda z, x, y, h, c: (z, x, (y + m) % 4, h, c))


ALONG = {
    "x": ("row", [[4 * z + x for x in range(4)] for z in range(4)]),
    "z": ("row", [[4 * z + x for z in range(4)] for x in range(4)]),
    "y": ("col", [[4 * y + j for y in range(4)] for j in range(4)]),
}


def exchange(values, line):
    axis, groups = ALONG[line]
    return lax.all_to_all(values, axis, 0, 0, axis_index_groups=groups, tiled=True)


def from_line(value, line):
    return exchange(jnp.broadcast_to(value[None], (4, *value.shape)), line)


def across(value):
    return route(value, lambda z, x, y, h, c: (z, x, y, h ^ 1, c))


def core_swap(value):
    return route(value, lambda z, x, y, h, c: (z, x, y, h, c ^ 1))


def after(value, *others):
    return lax.optimization_barrier((value, *others))[0]


def local(
    homolog_matrix,
    contact_matrix,
    seqs,
    residues,
    tensor_product_matrices,
    tensor_product_final,
    mixing_value_gate_matrix,
    mixing_logit_matrix,
    mixing_final_matrix,
    feedforward_gate_expand,
    feedforward_shrink_matrix,
):
    homolog = jnp.swapaxes(homolog_matrix, 1, 2)
    left, shared = prologue(seqs, residues, homolog, tensor_product_matrices[0])
    product_weight, value_weight, gate_weight, mixing_weight = arrange_weights(
        tensor_product_final[0], mixing_value_gate_matrix[0], mixing_final_matrix[0].T
    )

    halves = jnp.stack([
        route(left, lambda z, x, y, h, c, u=u: (y, 2 * h + c, z, (x >> 1) ^ u, x & 1)) for u in range(2)
    ])
    shared = jnp.stack([shared] + [along_z(shared, m) for m in (1, 2, 3)])
    column = shared[:, 16:]
    left_half = jnp.stack([halves] + [along_y(halves, m) for m in (1, 2, 3)])
    right = [column] + [along_x(column, m) for m in (1, 3, 2)]
    right[2], right[3] = right[3], right[2]
    left_all = [left_half, core_swap(left_half)]
    group = after(shared[:, :16], *left_all, *right)
    group = jnp.stack([group, across(group)])

    contact, weights = outer(
        seqs, residues, left_all, right, contact_matrix, product_weight, mixing_logit_matrix[0].T
    )
    group = after(group, weights)
    behind, ahead = along_y(group, 1), along_y(group, 3)
    weights = route(weights, lambda z, x, y, h, c: (y, 2 * h + c, z, x >> 1, x & 1))
    pair = transition(contact, feedforward_gate_expand[0], feedforward_shrink_matrix[0])
    weights, behind, ahead, pair = lax.optimization_barrier((weights, behind, ahead, pair))
    weights = jnp.stack([weights[0]] + [along_z(weights[v], v) for v in (1, 2, 3)])
    opposite = jnp.stack([along_y(behind[0], 1), along_y(ahead[1], 3)])
    weights, opposite = lax.optimization_barrier((weights, opposite))
    weights = [weights] + [along_x(weights, m) for m in (1, 3, 2)]
    weights[2], weights[3] = weights[3], weights[2]
    everyone = jnp.stack([group, behind, opposite, ahead])
    everyone = [everyone, core_swap(everyone)]
    own, *others = average(weights, everyone, value_weight, gate_weight, mixing_weight)
    others = [along_z(part, 4 - v) for v, part in zip((1, 2, 3), others)]
    msa = epilogue([own] + others, homolog)
    return jnp.swapaxes(msa, 1, 2), pair


def solution(mesh):
    split = jax.sharding.PartitionSpec("row", "col", None)
    whole = jax.sharding.PartitionSpec()
    return jax.shard_map(
        local, mesh=mesh, in_specs=(split, split) + (whole,) * 9, out_specs=(split, split), check_vma=False
    )
```

time: 218 us -> 130 us (0.60)
  waiting for transfers between devices: 71.9 us -> 32.2 us
  local copies, waits for them, and re-layouts: 24.2 us -> 5.71 us
  Pallas kernels: 48.2 us -> 33.5 us
  between operations: 15.6 us -> 2.17 us
    ppermute x2 -> x28, starting transfers between devices: 7.77 us -> 55.6 us  [route(): return lax.ppermute(value, ('row', 'col'), pairs)]
    all_to_all x3 -> x0, starting transfers between devices: 47.6 us -> none  [from_everyone(): lax.all_to_all(jnp.broadcast_to(value[None], (lax.axis_size(axis), *value...]
    all_gather x1 -> x0, waiting for transfers between devices: 42.1 us -> none  [local(): everyone = lax.all_gather(normed, 'col', tiled=True)]
    ppermute x2 -> x28, waiting for transfers between devices: 5.58 us -> 32.2 us  [route(): return lax.ppermute(value, ('row', 'col'), pairs)]
    all_to_all x3 -> x0, waiting for transfers between devices: 23.6 us -> none  [from_everyone(): lax.all_to_all(jnp.broadcast_to(value[None], (lax.axis_size(axis), *value...]
    pallas_call x4 -> x6, Pallas kernels: 48.2 us -> 33.5 us  [the longest x1 15.4 us: outer(): call(outer_body, 2, (80 // ROWS,), [full((4, 2, 8, 2560))] * 2 + [full((4...]
    mul x14 -> x0, local copies, waits for them, and re-layouts: 8.14 us -> none  [spread(): eye[None, :, None, :, None] * weight[:, None, :, None, :]]
    unnamed x33 -> x22, local copies, waits for them, and re-layouts: 10.4 us -> 5.66 us
  transfers between devices with their start and end apart: 6 -> 28, of which waited for: 5 -> 12; matrix products, arithmetic and copies ran while one was open for 5% -> 0% of each run, Pallas kernels for 5% -> 21%
where the time goes in v2:
time: 130 us
  starting transfers between devices  55.6 us (43%)
  Pallas kernels  33.5 us (26%)
  waiting for transfers between devices  32.2 us (25%)
  local copies, waits for them, and re-layouts  5.71 us (4%)
  between operations  2.17 us (2%)
    ppermute x28, starting transfers between devices, route(): return lax.ppermute(value, ('row', 'col'), pairs)  55.6 us
    ppermute x28, waiting for transfers between devices, route(): return lax.ppermute(value, ('row', 'col'), pairs)  32.2 us
    pallas_call x1, Pallas kernels, outer(): call(outer_body, 2, (80 // ROWS,), [full((4, 2, 8, 2560))] * 2 + [full((4...  15.4 us
    pallas_call x1, Pallas kernels, transition(): call(transition_body, 0, (10,), [block, full((128, 1024)), full((512, 128...  10.6 us
    unnamed x22, local copies, waits for them, and re-layouts  5.66 us
    pallas_call x1, Pallas kernels, average(): call(average_body, 0, (1,), [full((4, 160, 128))] * 4 + [full((4, 2, 4, 1...  5.18 us
  transfers between devices with their start and end apart: 28, of which 12 were waited for; matrix products, arithmetic and copies ran while one was open for 0% of the time, Pallas kernels for 21%

profile of v2, /device:TPU:1, one launch (start us, length us, event | category | flops | bytes accessed | tf_op | source)
XLA Modules:
  0.0 129.7 jit_solution(15395237989181287574)
XLA Ops:
  4.2 9.3 %collective-permute-start.1 = (bf16[8,2560]{1,0:T(8,128)(2,1)S(1)}, bf16[8,2560]{1,0:T(8,128)(2,1)S(1)}, u32[]{:S(2)}, u32[]{:S(2)}) collective-permute-start(bf16[8,2560]{1,0:T(8,128)(2,1)S(1)} %get-tuple-element.22), channel_id=1, source_target_pairs={{0,2},{1,18},{2,34},{3,50},{4,66},{5,82},{6,98},{7,114},{8,130},{9... | collective-permute-start | bytes 122888 | tf_op jit(solution)/shard_map/ppermute | solution.py:320
  13.5 1.9 %collective-permute-start = (bf16[8,2560]{1,0:T(8,128)(2,1)S(1)}, bf16[8,2560]{1,0:T(8,128)(2,1)S(1)}, u32[]{:S(2)}, u32[]{:S(2)}) collective-permute-start(bf16[8,2560]{1,0:T(8,128)(2,1)S(1)} %get-tuple-element.22), channel_id=1, source_target_pairs={{0,0},{1,16},{2,32},{3,48},{4,64},{5,80},{6,96},{7,112},{8,128},{9... | collective-permute-start | bytes 122888 | tf_op jit(solution)/shard_map/ppermute | solution.py:320
  15.4 3.8 %collective-permute-start.8 = (bf16[24,2560]{1,0:T(8,128)(2,1)S(1)}, bf16[24,2560]{1,0:T(8,128)(2,1)S(1)}, u32[]{:S(2)}, u32[]{:S(2)}) collective-permute-start(bf16[24,2560]{1,0:T(8,128)(2,1)S(1)} %get-tuple-element.23), channel_id=1, source_target_pairs={{0,192},{1,193},{2,194},{3,195},{4,196},{5,197},{6,198},{7,199},{8... | collective-permute-start | bytes 368648 | tf_op jit(solution)/shard_map/ppermute | solution.py:320
  23.9 2.7 %collective-permute-start.3 = (bf16[2,8,2560]{2,1,0:T(8,128)(2,1)S(1)}, bf16[2,8,2560]{2,1,0:T(8,128)(2,1)S(1)}, u32[]{:S(2)}, u32[]{:S(2)}) collective-permute-start(bf16[2,8,2560]{2,1,0:T(8,128)(2,1)S(1)} %get-tuple-element.47), channel_id=1, source_target_pairs={{0,8},{1,9},{2,10},{3,11},{4,12},{5,13},{6,14},{7,15},{8,0},{9,1},... | collective-permute-start | bytes 245768 | tf_op jit(solution)/shard_map/ppermute | solution.py:320
  26.6 2.7 %collective-permute-start.4 = (bf16[2,8,2560]{2,1,0:T(8,128)(2,1)S(1)}, bf16[2,8,2560]{2,1,0:T(8,128)(2,1)S(1)}, u32[]{:S(2)}, u32[]{:S(2)}) collective-permute-start(bf16[2,8,2560]{2,1,0:T(8,128)(2,1)S(1)} %get-tuple-element.47), channel_id=1, source_target_pairs={{0,12},{1,13},{2,14},{3,15},{4,0},{5,1},{6,2},{7,3},{8,4},{9,5},{1... | collective-permute-start | bytes 245768 | tf_op jit(solution)/shard_map/ppermute | solution.py:320
  29.3 3.0 %collective-permute-done.7 = bf16[24,2560]{1,0:T(8,128)(2,1)S(1)} collective-permute-done((bf16[24,2560]{1,0:T(8,128)(2,1)S(1)}, bf16[24,2560]{1,0:T(8,128)(2,1)S(1)}, u32[]{:S(2)}, u32[]{:S(2)}) %collective-permute-start.7) | collective-permute-done | bytes 122912 | tf_op jit(solution)/shard_map/ppermute | solution.py:320
  32.3 1.6 %collective-permute-start.11 = (bf16[4,8,2560]{2,1,0:T(8,128)(2,1)S(1)}, bf16[4,8,2560]{2,1,0:T(8,128)(2,1)S(1)}, u32[]{:S(2)}, u32[]{:S(2)}) collective-permute-start(bf16[4,8,2560]{2,1,0:T(8,128)(2,1)S(1)} %pad_maximum_fusion.7.right_a), channel_id=1, source_target_pairs={{0,48},{1,49},{2,50},{3,51},{4,52},{5,53},{6,54},{7,55},{8,56},{9,... | collective-permute-start | bytes 491528 | tf_op jit(solution)/shard_map/ppermute | solution.py:320
  34.6 2.4 %collective-permute-start.5 = (bf16[4,2,8,2560]{3,2,1,0:T(8,128)(2,1)S(1)}, bf16[4,2,8,2560]{3,2,1,0:T(8,128)(2,1)S(1)}, u32[]{:S(2)}, u32[]{:S(2)}) collective-permute-start(bf16[4,2,8,2560]{3,2,1,0:T(8,128)(2,1)S(1)} %pad_maximum_fusion.6.left_a), channel_id=1, source_target_pairs={{0,1},{1,0},{2,3},{3,2},{4,5},{5,4},{6,7},{7,6},{8,9},{9,8},{10,11... | collective-permute-start | bytes 983048 | tf_op jit(solution)/shard_map/ppermute | solution.py:320
  37.5 2.2 %collective-permute-done.10.right_c = bf16[4,8,2560]{2,1,0:T(8,128)(2,1)S(1)} collective-permute-done((bf16[4,8,2560]{2,1,0:T(8,128)(2,1)S(1)}, bf16[4,8,2560]{2,1,0:T(8,128)(2,1)S(1)}, u32[]{:S(2)}, u32[]{:S(2)}) %collective-permute-start.10) | collective-permute-done | bytes 163872 | tf_op jit(solution)/shard_map/ppermute | solution.py:320
  39.7 4.7 %collective-permute-done.9.right_b = bf16[4,8,2560]{2,1,0:T(8,128)(2,1)S(1)} collective-permute-done((bf16[4,8,2560]{2,1,0:T(8,128)(2,1)S(1)}, bf16[4,8,2560]{2,1,0:T(8,128)(2,1)S(1)}, u32[]{:S(2)}, u32[]{:S(2)}) %collective-permute-start.9) | collective-permute-done | bytes 163872 | tf_op jit(solution)/shard_map/ppermute | solution.py:320
  44.4 15.4 %outer_body.1 = (bf16[80,80,128]{2,1,0:T(8,128)(2,1)S(1)}, bf16[4,160,128]{2,1,0:T(8,128)(2,1)S(1)}) custom-call(s32[1]{0:T(128)S(6)} %copy.13.seqs, s32[1]{0:T(128)S(6)} %copy.14.residues, bf16[4,2,8,2560]{3,2,1,0:T(8,128)(2,1)S(1)} %pad_maximum_fusion.6.left_a, bf16[4,2,8,2560]{3,2,1,0:T(8,128)(2,1)S(1)} %collective-permute-done.5.left_b, ...), custom_call_target="tpu_custom_call" | custom-call | flops 12000000000 | bytes 6000000 | tf_op jit(solution)/shard_map/outer_body/pallas_call | solution.py:187
  59.9 3.0 %collective-permute-start.15 = (bf16[2,4,16,2560]{3,2,1,0:T(8,128)(2,1)S(1)}, bf16[2,4,16,2560]{3,2,1,0:T(8,128)(2,1)S(1)}, u32[]{:S(2)}, u32[]{:S(2)}) collective-permute-start(bf16[2,4,16,2560]{3,2,1,0:T(8,128)(2,1)S(1)} %pad_maximum_fusion.1), channel_id=1, source_target_pairs={{0,12},{1,13},{2,14},{3,15},{4,0},{5,1},{6,2},{7,3},{8,4},{9,5},{1... | collective-permute-start | bytes 1966088 | tf_op jit(solution)/shard_map/ppermute | solution.py:320
  64.3 2.0 %collective-permute-start.12 = (bf16[4,160,128]{2,1,0:T(8,128)(2,1)S(1)}, bf16[4,160,128]{2,1,0:T(8,128)(2,1)S(1)}, u32[]{:S(2)}, u32[]{:S(2)}) collective-permute-start(bf16[4,160,128]{2,1,0:T(8,128)(2,1)S(1)} %get-tuple-element.25), channel_id=1, source_target_pairs={{0,0},{1,16},{2,32},{3,48},{4,64},{5,80},{6,96},{7,112},{8,128},{9... | collective-permute-start | bytes 491528 | tf_op jit(solution)/shard_map/ppermute | solution.py:320
  66.4 10.6 %transition_body.1 = bf16[80,80,128]{2,1,0:T(8,128)(2,1)} custom-call(bf16[80,80,128]{2,1,0:T(8,128)(2,1)S(1)} %get-tuple-element.28.contact, bf16[128,1024]{1,0:T(8,128)(2,1)S(1)} %bitcast.52, bf16[512,128]{1,0:T(8,128)(2,1)S(1)} %bitcast.53), custom_call_target="tpu_custom_call" | custom-call | flops 5000000000 | bytes 3300000 | tf_op jit(solution)/shard_map/transition_body/pallas_call | solution.py:212
  77.0 5.4 %collective-permute-done.12 = bf16[4,160,128]{2,1,0:T(8,128)(2,1)S(1)} collective-permute-done((bf16[4,160,128]{2,1,0:T(8,128)(2,1)S(1)}, bf16[4,160,128]{2,1,0:T(8,128)(2,1)S(1)}, u32[]{:S(2)}, u32[]{:S(2)}) %collective-permute-start.12) | collective-permute-done | bytes 163872 | tf_op jit(solution)/shard_map/ppermute | solution.py:320
  82.5 1.8 %collective-permute-start.19 = (bf16[4,16,2560]{2,1,0:T(8,128)(2,1)S(1)}, bf16[4,16,2560]{2,1,0:T(8,128)(2,1)S(1)}, u32[]{:S(2)}, u32[]{:S(2)}) collective-permute-start(bf16[4,16,2560]{2,1,0:T(8,128)(2,1)S(1)} %slice_bitcast_fusion.1), channel_id=1, source_target_pairs={{0,4},{1,5},{2,6},{3,7},{4,8},{5,9},{6,10},{7,11},{8,12},{9,13},{1... | collective-permute-start | bytes 983048 | tf_op jit(solution)/shard_map/ppermute | solution.py:320
  85.0 10.1 %collective-permute-start.17 = (bf16[160,128]{1,0:T(8,128)(2,1)S(1)}, bf16[160,128]{1,0:T(8,128)(2,1)S(1)}, u32[]{:S(2)}, u32[]{:S(2)}) collective-permute-start(bf16[160,128]{1,0:T(8,128)(2,1)S(1)} %get-tuple-element.44), channel_id=1, source_target_pairs={{0,128},{1,129},{2,130},{3,131},{4,132},{5,133},{6,134},{7,135},{8... | collective-permute-start | bytes 122888 | tf_op jit(solution)/shard_map/ppermute | solution.py:320
  97.9 1.9 %collective-permute-done.16 = bf16[160,128]{1,0:T(8,128)(2,1)S(1)} collective-permute-done((bf16[160,128]{1,0:T(8,128)(2,1)S(1)}, bf16[160,128]{1,0:T(8,128)(2,1)S(1)}, u32[]{:S(2)}, u32[]{:S(2)}) %collective-permute-start.16) | collective-permute-done | bytes 40992 | tf_op jit(solution)/shard_map/ppermute | solution.py:320
  104.4 3.1 %collective-permute-done.23.part_d = bf16[4,160,128]{2,1,0:T(8,128)(2,1)S(1)} collective-permute-done((bf16[4,160,128]{2,1,0:T(8,128)(2,1)S(1)}, bf16[4,160,128]{2,1,0:T(8,128)(2,1)S(1)}, u32[]{:S(2)}, u32[]{:S(2)}) %collective-permute-start.23) | collective-permute-done | bytes 163872 | tf_op jit(solution)/shard_map/ppermute | solution.py:320
  107.5 2.5 %collective-permute-done.22.part_c = bf16[4,160,128]{2,1,0:T(8,128)(2,1)S(1)} collective-permute-done((bf16[4,160,128]{2,1,0:T(8,128)(2,1)S(1)}, bf16[4,160,128]{2,1,0:T(8,128)(2,1)S(1)}, u32[]{:S(2)}, u32[]{:S(2)}) %collective-permute-start.22) | collective-permute-done | bytes 163872 | tf_op jit(solution)/shard_map/ppermute | solution.py:320
  110.0 4.2 %collective-permute-done.21.part_b = bf16[4,160,128]{2,1,0:T(8,128)(2,1)S(1)} collective-permute-done((bf16[4,160,128]{2,1,0:T(8,128)(2,1)S(1)}, bf16[4,160,128]{2,1,0:T(8,128)(2,1)S(1)}, u32[]{:S(2)}, u32[]{:S(2)}) %collective-permute-start.21) | collective-permute-done | bytes 163872 | tf_op jit(solution)/shard_map/ppermute | solution.py:320
  115.7 5.2 %average_body.1 = (f32[48,256]{1,0:T(8,128)S(1)}, f32[48,256]{1,0:T(8,128)S(1)}, f32[48,256]{1,0:T(8,128)S(1)}, f32[48,256]{1,0:T(8,128)S(1)}) custom-call(bf16[4,160,128]{2,1,0:T(8,128)(2,1)S(1)} %pad_maximum_fusion.8.part_a, bf16[4,160,128]{2,1,0:T(8,128)(2,1)S(1)} %collective-permute-done.21.part_b, ...), custom_call_target="tpu_custom_call" | custom-call | flops 3000000000 | bytes 8000000 | tf_op jit(solution)/shard_map/average_body/pallas_call | solution.py:276
  121.1 3.0 %collective-permute-start.26 = (f32[48,256]{1,0:T(8,128)S(1)}, f32[48,256]{1,0:T(8,128)S(1)}, u32[]{:S(2)}, u32[]{:S(2)}) collective-permute-start(f32[48,256]{1,0:T(8,128)S(1)} %get-tuple-element.39), channel_id=1, source_target_pairs={{0,128},{1,129},{2,130},{3,131},{4,132},{5,133},{6,134},{7,135},{8... | collective-permute-start | bytes 147464 | tf_op jit(solution)/shard_map/ppermute | solution.py:320
  126.1 2.8 %collective-permute-done.27.part_d = f32[48,256]{1,0:T(8,128)S(1)} collective-permute-done((f32[48,256]{1,0:T(8,128)S(1)}, f32[48,256]{1,0:T(8,128)S(1)}, u32[]{:S(2)}, u32[]{:S(2)}) %collective-permute-start.27) | collective-permute-done | bytes 49184 | tf_op jit(solution)/shard_map/ppermute | solution.py:320
  (71 shorter events, 22.3 us)
Async XLA Ops:
  4.2 19.7 %collective-permute-start.1 = (bf16[8,2560]{1,0:T(8,128)(2,1)S(1)}, bf16[8,2560]{1,0:T(8,128)(2,1)S(1)}, u32[]{:S(2)}, u32[]{:S(2)}) collective-permute-start(bf16[8,2560]{1,0:T(8,128)(2,1)S(1)} %get-tuple-element.22), channel_id=1, source_target_pairs={{0,2},{1,18},{2,34},{3,50},{4,66},{5,82},{6,98},{7,114},{8,130},{9... | collective-permute-start | bytes 122888 | tf_op jit(solution)/shard_map/ppermute | solution.py:320
  13.5 10.4 %collective-permute-start = (bf16[8,2560]{1,0:T(8,128)(2,1)S(1)}, bf16[8,2560]{1,0:T(8,128)(2,1)S(1)}, u32[]{:S(2)}, u32[]{:S(2)}) collective-permute-start(bf16[8,2560]{1,0:T(8,128)(2,1)S(1)} %get-tuple-element.22), channel_id=1, source_target_pairs={{0,0},{1,16},{2,32},{3,48},{4,64},{5,80},{6,96},{7,112},{8,128},{9... | collective-permute-start | bytes 122888 | tf_op jit(solution)/shard_map/ppermute | solution.py:320
  15.4 11.2 %collective-permute-start.8 = (bf16[24,2560]{1,0:T(8,128)(2,1)S(1)}, bf16[24,2560]{1,0:T(8,128)(2,1)S(1)}, u32[]{:S(2)}, u32[]{:S(2)}) collective-permute-start(bf16[24,2560]{1,0:T(8,128)(2,1)S(1)} %get-tuple-element.23), channel_id=1, source_target_pairs={{0,192},{1,193},{2,194},{3,195},{4,196},{5,197},{6,198},{7,199},{8... | collective-permute-start | bytes 368648 | tf_op jit(solution)/shard_map/ppermute | solution.py:320
  19.2 13.1 %collective-permute-start.7 = (bf16[24,2560]{1,0:T(8,128)(2,1)S(1)}, bf16[24,2560]{1,0:T(8,128)(2,1)S(1)}, u32[]{:S(2)}, u32[]{:S(2)}) collective-permute-start(bf16[24,2560]{1,0:T(8,128)(2,1)S(1)} %get-tuple-element.23), channel_id=1, source_target_pairs={{0,128},{1,129},{2,130},{3,131},{4,132},{5,133},{6,134},{7,135},{8... | collective-permute-start | bytes 368648 | tf_op jit(solution)/shard_map/ppermute | solution.py:320
  19.2 13.1 %collective-permute-start.6 = (bf16[24,2560]{1,0:T(8,128)(2,1)S(1)}, bf16[24,2560]{1,0:T(8,128)(2,1)S(1)}, u32[]{:S(2)}, u32[]{:S(2)}) collective-permute-start(bf16[24,2560]{1,0:T(8,128)(2,1)S(1)} %get-tuple-element.23), channel_id=1, source_target_pairs={{0,64},{1,65},{2,66},{3,67},{4,68},{5,69},{6,70},{7,71},{8,72},{9,... | collective-permute-start | bytes 368648 | tf_op jit(solution)/shard_map/ppermute | solution.py:320
  23.9 10.0 %collective-permute-start.3 = (bf16[2,8,2560]{2,1,0:T(8,128)(2,1)S(1)}, bf16[2,8,2560]{2,1,0:T(8,128)(2,1)S(1)}, u32[]{:S(2)}, u32[]{:S(2)}) collective-permute-start(bf16[2,8,2560]{2,1,0:T(8,128)(2,1)S(1)} %get-tuple-element.47), channel_id=1, source_target_pairs={{0,8},{1,9},{2,10},{3,11},{4,12},{5,13},{6,14},{7,15},{8,0},{9,1},... | collective-permute-start | bytes 245768 | tf_op jit(solution)/shard_map/ppermute | solution.py:320
  26.6 8.0 %collective-permute-start.2 = (bf16[2,8,2560]{2,1,0:T(8,128)(2,1)S(1)}, bf16[2,8,2560]{2,1,0:T(8,128)(2,1)S(1)}, u32[]{:S(2)}, u32[]{:S(2)}) collective-permute-start(bf16[2,8,2560]{2,1,0:T(8,128)(2,1)S(1)} %get-tuple-element.47), channel_id=1, source_target_pairs={{0,4},{1,5},{2,6},{3,7},{4,8},{5,9},{6,10},{7,11},{8,12},{9,13},{1... | collective-permute-start | bytes 245768 | tf_op jit(solution)/shard_map/ppermute | solution.py:320
  26.6 8.0 %collective-permute-start.4 = (bf16[2,8,2560]{2,1,0:T(8,128)(2,1)S(1)}, bf16[2,8,2560]{2,1,0:T(8,128)(2,1)S(1)}, u32[]{:S(2)}, u32[]{:S(2)}) collective-permute-start(bf16[2,8,2560]{2,1,0:T(8,128)(2,1)S(1)} %get-tuple-element.47), channel_id=1, source_target_pairs={{0,12},{1,13},{2,14},{3,15},{4,0},{5,1},{6,2},{7,3},{8,4},{9,5},{1... | collective-permute-start | bytes 245768 | tf_op jit(solution)/shard_map/ppermute | solution.py:320
  32.3 5.2 %collective-permute-start.11 = (bf16[4,8,2560]{2,1,0:T(8,128)(2,1)S(1)}, bf16[4,8,2560]{2,1,0:T(8,128)(2,1)S(1)}, u32[]{:S(2)}, u32[]{:S(2)}) collective-permute-start(bf16[4,8,2560]{2,1,0:T(8,128)(2,1)S(1)} %pad_maximum_fusion.7.right_a), channel_id=1, source_target_pairs={{0,48},{1,49},{2,50},{3,51},{4,52},{5,53},{6,54},{7,55},{8,56},{9,... | collective-permute-start | bytes 491528 | tf_op jit(solution)/shard_map/ppermute | solution.py:320
  33.9 5.8 %collective-permute-start.10 = (bf16[4,8,2560]{2,1,0:T(8,128)(2,1)S(1)}, bf16[4,8,2560]{2,1,0:T(8,128)(2,1)S(1)}, u32[]{:S(2)}, u32[]{:S(2)}) collective-permute-start(bf16[4,8,2560]{2,1,0:T(8,128)(2,1)S(1)} %pad_maximum_fusion.7.right_a), channel_id=1, source_target_pairs={{0,32},{1,33},{2,34},{3,35},{4,36},{5,37},{6,38},{7,39},{8,40},{9,... | collective-permute-start | bytes 491528 | tf_op jit(solution)/shard_map/ppermute | solution.py:320
  33.9 10.5 %collective-permute-start.9 = (bf16[4,8,2560]{2,1,0:T(8,128)(2,1)S(1)}, bf16[4,8,2560]{2,1,0:T(8,128)(2,1)S(1)}, u32[]{:S(2)}, u32[]{:S(2)}) collective-permute-start(bf16[4,8,2560]{2,1,0:T(8,128)(2,1)S(1)} %pad_maximum_fusion.7.right_a), channel_id=1, source_target_pairs={{0,16},{1,17},{2,18},{3,19},{4,20},{5,21},{6,22},{7,23},{8,24},{9,... | collective-permute-start | bytes 491528 | tf_op jit(solution)/shard_map/ppermute | solution.py:320
  34.6 9.7 %collective-permute-start.5 = (bf16[4,2,8,2560]{3,2,1,0:T(8,128)(2,1)S(1)}, bf16[4,2,8,2560]{3,2,1,0:T(8,128)(2,1)S(1)}, u32[]{:S(2)}, u32[]{:S(2)}) collective-permute-start(bf16[4,2,8,2560]{3,2,1,0:T(8,128)(2,1)S(1)} %pad_maximum_fusion.6.left_a), channel_id=1, source_target_pairs={{0,1},{1,0},{2,3},{3,2},{4,5},{5,4},{6,7},{7,6},{8,9},{9,8},{10,11... | collective-permute-start | bytes 983048 | tf_op jit(solution)/shard_map/ppermute | solution.py:320
  44.4 15.5 %collective-permute-start.13 = (bf16[4,16,2560]{2,1,0:T(8,128)(2,1)S(1)}, bf16[4,16,2560]{2,1,0:T(8,128)(2,1)S(1)}, u32[]{:S(2)}, u32[]{:S(2)}) collective-permute-start(bf16[4,16,2560]{2,1,0:T(8,128)(2,1)S(1)} %pad_maximum_fusion.3), channel_id=1, source_target_pairs={{0,2},{1,3},{2,0},{3,1},{4,6},{5,7},{6,4},{7,5},{8,10},{9,11},{10,... | collective-permute-start | bytes 983048 | tf_op jit(solution)/shard_map/ppermute | solution.py:320
  59.9 22.5 %collective-permute-start.15 = (bf16[2,4,16,2560]{3,2,1,0:T(8,128)(2,1)S(1)}, bf16[2,4,16,2560]{3,2,1,0:T(8,128)(2,1)S(1)}, u32[]{:S(2)}, u32[]{:S(2)}) collective-permute-start(bf16[2,4,16,2560]{3,2,1,0:T(8,128)(2,1)S(1)} %pad_maximum_fusion.1), channel_id=1, source_target_pairs={{0,12},{1,13},{2,14},{3,15},{4,0},{5,1},{6,2},{7,3},{8,4},{9,5},{1... | collective-permute-start | bytes 1966088 | tf_op jit(solution)/shard_map/ppermute | solution.py:320
  62.9 19.5 %collective-permute-start.14 = (bf16[2,4,16,2560]{3,2,1,0:T(8,128)(2,1)S(1)}, bf16[2,4,16,2560]{3,2,1,0:T(8,128)(2,1)S(1)}, u32[]{:S(2)}, u32[]{:S(2)}) collective-permute-start(bf16[2,4,16,2560]{3,2,1,0:T(8,128)(2,1)S(1)} %pad_maximum_fusion.1), channel_id=1, source_target_pairs={{0,4},{1,5},{2,6},{3,7},{4,8},{5,9},{6,10},{7,11},{8,12},{9,13},{1... | collective-permute-start | bytes 1966088 | tf_op jit(solution)/shard_map/ppermute | solution.py:320
  64.3 18.1 %collective-permute-start.12 = (bf16[4,160,128]{2,1,0:T(8,128)(2,1)S(1)}, bf16[4,160,128]{2,1,0:T(8,128)(2,1)S(1)}, u32[]{:S(2)}, u32[]{:S(2)}) collective-permute-start(bf16[4,160,128]{2,1,0:T(8,128)(2,1)S(1)} %get-tuple-element.25), channel_id=1, source_target_pairs={{0,0},{1,16},{2,32},{3,48},{4,64},{5,80},{6,96},{7,112},{8,128},{9... | collective-permute-start | bytes 491528 | tf_op jit(solution)/shard_map/ppermute | solution.py:320
  82.4 17.4 %collective-permute-start.20 = (bf16[4,16,2560]{2,1,0:T(8,128)(2,1)S(1)}, bf16[4,16,2560]{2,1,0:T(8,128)(2,1)S(1)}, u32[]{:S(2)}, u32[]{:S(2)}) collective-permute-start(bf16[4,16,2560]{2,1,0:T(8,128)(2,1)S(1)} %slice_bitcast_fusion), channel_id=1, source_target_pairs={{0,12},{1,13},{2,14},{3,15},{4,0},{5,1},{6,2},{7,3},{8,4},{9,5},{1... | collective-permute-start | bytes 983048 | tf_op jit(solution)/shard_map/ppermute | solution.py:320
  82.5 17.3 %collective-permute-start.19 = (bf16[4,16,2560]{2,1,0:T(8,128)(2,1)S(1)}, bf16[4,16,2560]{2,1,0:T(8,128)(2,1)S(1)}, u32[]{:S(2)}, u32[]{:S(2)}) collective-permute-start(bf16[4,16,2560]{2,1,0:T(8,128)(2,1)S(1)} %slice_bitcast_fusion.1), channel_id=1, source_target_pairs={{0,4},{1,5},{2,6},{3,7},{4,8},{5,9},{6,10},{7,11},{8,12},{9,13},{1... | collective-permute-start | bytes 983048 | tf_op jit(solution)/shard_map/ppermute | solution.py:320
  84.3 12.2 %collective-permute-start.18 = (bf16[160,128]{1,0:T(8,128)(2,1)S(1)}, bf16[160,128]{1,0:T(8,128)(2,1)S(1)}, u32[]{:S(2)}, u32[]{:S(2)}) collective-permute-start(bf16[160,128]{1,0:T(8,128)(2,1)S(1)} %get-tuple-element.43), channel_id=1, source_target_pairs={{0,192},{1,193},{2,194},{3,195},{4,196},{5,197},{6,198},{7,199},{8... | collective-permute-start | bytes 122888 | tf_op jit(solution)/shard_map/ppermute | solution.py:320
  85.0 12.9 %collective-permute-start.17 = (bf16[160,128]{1,0:T(8,128)(2,1)S(1)}, bf16[160,128]{1,0:T(8,128)(2,1)S(1)}, u32[]{:S(2)}, u32[]{:S(2)}) collective-permute-start(bf16[160,128]{1,0:T(8,128)(2,1)S(1)} %get-tuple-element.44), channel_id=1, source_target_pairs={{0,128},{1,129},{2,130},{3,131},{4,132},{5,133},{6,134},{7,135},{8... | collective-permute-start | bytes 122888 | tf_op jit(solution)/shard_map/ppermute | solution.py:320
  100.3 13.9 %collective-permute-start.24 = (bf16[4,2,4,16,2560]{4,3,2,1,0:T(8,128)(2,1)S(1)}, bf16[4,2,4,16,2560]{4,3,2,1,0:T(8,128)(2,1)S(1)}, u32[]{:S(2)}, u32[]{:S(2)}) collective-permute-start(bf16[4,2,4,16,2560]{4,3,2,1,0:T(8,128)(2,1)S(1)} %pad_maximum_fusion.everyone_a), channel_id=1, source_target_pairs={{0,1},{1,0},{2,3},{3,2},{4,5},{5,4},{6,7},{7,6},{8,9},{9,8},{10,11... | collective-permute-start | bytes 7864328 | tf_op jit(solution)/shard_map/ppermute | solution.py:320
  101.8 5.8 %collective-permute-start.23 = (bf16[4,160,128]{2,1,0:T(8,128)(2,1)S(1)}, bf16[4,160,128]{2,1,0:T(8,128)(2,1)S(1)}, u32[]{:S(2)}, u32[]{:S(2)}) collective-permute-start(bf16[4,160,128]{2,1,0:T(8,128)(2,1)S(1)} %pad_maximum_fusion.8.part_a), channel_id=1, source_target_pairs={{0,48},{1,49},{2,50},{3,51},{4,52},{5,53},{6,54},{7,55},{8,56},{9,... | collective-permute-start | bytes 491528 | tf_op jit(solution)/shard_map/ppermute | solution.py:320
  103.0 7.0 %collective-permute-start.22 = (bf16[4,160,128]{2,1,0:T(8,128)(2,1)S(1)}, bf16[4,160,128]{2,1,0:T(8,128)(2,1)S(1)}, u32[]{:S(2)}, u32[]{:S(2)}) collective-permute-start(bf16[4,160,128]{2,1,0:T(8,128)(2,1)S(1)} %pad_maximum_fusion.8.part_a), channel_id=1, source_target_pairs={{0,32},{1,33},{2,34},{3,35},{4,36},{5,37},{6,38},{7,39},{8,40},{9,... | collective-permute-start | bytes 491528 | tf_op jit(solution)/shard_map/ppermute | solution.py:320
  103.5 10.7 %collective-permute-start.21 = (bf16[4,160,128]{2,1,0:T(8,128)(2,1)S(1)}, bf16[4,160,128]{2,1,0:T(8,128)(2,1)S(1)}, u32[]{:S(2)}, u32[]{:S(2)}) collective-permute-start(bf16[4,160,128]{2,1,0:T(8,128)(2,1)S(1)} %pad_maximum_fusion.8.part_a), channel_id=1, source_target_pairs={{0,16},{1,17},{2,18},{3,19},{4,20},{5,21},{6,22},{7,23},{8,24},{9,... | collective-permute-start | bytes 491528 | tf_op jit(solution)/shard_map/ppermute | solution.py:320
  (15 other events, 147.0 us)

commit v3 on v2

--- a/solution.py
+++ b/solution.py
@@ -47,7 +47,7 @@
     return jax.ShapeDtypeStruct(dims, dtype)
 
 
-def prologue_body(seqs, residues, homolog, weight, left_out, shared_out, left_rows, right_rows):
+def prologue_body(seqs, residues, homolog, weight, left_out, right_out, shared_out, left_rows, right_rows):
     row, col = lax.axis_index("row"), lax.axis_index("col")
     normed = normalize(homolog[...].astype(F32), 1)
     rounded = normed.astype(BF)
@@ -72,15 +72,17 @@
         left_out[:, q * 128 : (q + 1) * 128] = jnp.where(ok, piece, 0.0).astype(BF)
     ok = seq_ok & (col * 80 + lane < residues[0])
     pieces = [jnp.where(ok, right_rows[:, d, :], 0.0)[:, :80] for d in range(32)]
-    shared_out[16:, :] = jnp.concatenate(pieces, axis=1).astype(BF)
+    pieces = jnp.concatenate(pieces, axis=1).astype(BF)
+    right_out[...] = pieces
+    shared_out[16:, :] = pieces
 
 
 def prologue(seqs, residues, homolog, weight):
     return call(
         prologue_body, 2, (1,),
         [full((8, 64, 80)), full((64, 64))],
-        [full((8, 2560)), full((24, 2560))],
-        [shaped(BF, 8, 2560), shaped(BF, 24, 2560)],
+        [full((8, 2560)), full((8, 2560)), full((24, 2560))],
+        [shaped(BF, 8, 2560), shaped(BF, 8, 2560), shaped(BF, 24, 2560)],
         [pltpu.VMEM((8, 80, 128), F32), pltpu.VMEM((8, 32, 128), F32)],
         (10**8, 4 * 10**5, 10**4),
     )(seqs, residues, homolog, weight)
@@ -127,7 +129,7 @@
         left_t[...] = jnp.transpose(flat[...]).astype(BF)
         for m, part in enumerate((right_a, right_b, right_c, right_d)):
             for v in range(4):
-                z = ((row >> 2) - v) & 3
+                z = (row >> 2) ^ v
                 x = (row - m) & 3
                 place = ((col ^ x) & 1) * 8 + (((col >> 2) - z) & 3) * 2 + (((col >> 1) ^ (x >> 1)) & 1)
                 flat[pl.ds(pl.multiple_of(place * 8, 8), 8), :] = part[v].astype(F32)
@@ -178,8 +180,8 @@
 
     @pl.when(step == 80 // ROWS - 1)
     def _():
-        for q in range(4):
-            weights_out[q] = expo[pl.ds((((col >> 2) + q) & 3) * 20, 20)].reshape(160, 128).astype(BF)
+        for q in range(2):
+            weights_out[q] = expo[pl.ds((((col >> 2) + q) & 1) * 40, 40)].reshape(320, 128).astype(BF)
 
 
 def outer(seqs, residues, left, right, contact, final_weight, logit_weight):
@@ -187,8 +189,8 @@
     return call(
         outer_body, 2, (80 // ROWS,),
         [full((4, 2, 8, 2560))] * 2 + [full((4, 8, 2560))] * 4 + [block, full((128, 1024)), full((8, 128))],
-        [block, full((4, 160, 128))],
-        [shaped(BF, 80, 80, 128), shaped(BF, 4, 160, 128)],
+        [block, full((2, 320, 128))],
+        [shaped(BF, 80, 80, 128), shaped(BF, 2, 320, 128)],
         [
             pltpu.VMEM((2560, 128), BF), pltpu.VMEM((128, 4096), BF), pltpu.VMEM((1024, 128 * ROWS), BF),
             pltpu.VMEM((80, 8, 128), F32), pltpu.VMEM((128, 2560), F32),
@@ -217,16 +219,19 @@
     )(contact, up_weight, down_weight)
 
 
-def average_body(part_a, part_b, part_c, part_d, everyone_a, everyone_b, value_weight, gate_weight, final_weight,
-                 out_a, out_b, out_c, out_d, scaled, mixed, normed):
+def average_body(part_a, part_b, part_c, part_d, part_e, everyone_a, everyone_b, value_weight, gate_weight, final_weight,
+                 out_a, out_b, scaled, mixed, normed):
     row, col = lax.axis_index("row"), lax.axis_index("col")
-    parts = (part_a, part_b, part_c, part_d)
+    parts = (part_a, part_b, (part_c.at[0], part_c.at[1], part_d.at[0], part_d.at[1]), part_e)
     blocks = [(x, z) for x in range(4) for z in range(4)]
-    lane = lax.broadcasted_iota(jnp.int32, (160, 128), 1)
+    lane = lax.broadcasted_iota(jnp.int32, (320, 128), 1)
+
+    def block(x, z):
+        return (parts[x][z][...] if x == 2 else parts[x][z]).astype(F32)
 
     def stat(x, z, k):
         here = (lane >= 80 + 3 * k) & (lane < 83 + 3 * k)
-        return jnp.sum(jnp.where(here, parts[x][z].astype(F32), 0.0), axis=-1, keepdims=True)
+        return jnp.sum(jnp.where(here, block(x, z), 0.0), axis=-1, keepdims=True)
 
     peaks = [stat(x, z, 0) for x, z in blocks]
     peak = peaks[0]
@@ -236,62 +241,60 @@
     total = sum(f * stat(x, z, 1) for f, (x, z) in zip(factors, blocks))
     inverse = 1.0 / total
     for factor, (x, z) in zip(factors, blocks):
-        far_z = ((row >> 2) - z) & 3
+        far_z = (row >> 2) ^ z
         far_x = (row - x) & 3
         place = ((col ^ far_x) & 1) * 8 + (((col >> 2) - far_z) & 3) * 2 + (((col >> 1) ^ (far_x >> 1)) & 1)
-        scaled[place] = parts[x][z].astype(F32) * (factor * inverse)
+        scaled[place] = block(x, z) * (factor * inverse)
     for w, everyone in enumerate((everyone_a, everyone_b)):
         for v in range(4):
             for u in range(2):
                 for k in range(5):
                     start = (w * 8 + v * 2 + u) * 80 + k * 16
-                    for z in range(4):
+                    for z in range(2):
                         normed[start : start + 16, z * 512 : (z + 1) * 512] = everyone[v, u, z, :, k * 512 : (k + 1) * 512]
     sums = None
     for w in range(2):
         rows = jnp.concatenate([scaled[w * 8 + k][:, :80] for k in range(8)], axis=1).astype(BF)
         term = jnp.dot(rows, normed[w * 640 : (w + 1) * 640, :], preferred_element_type=F32)
         sums = term if sums is None else sums + term
-    mixed[...] = sums.reshape(20, 8, 2048)
-    pick = lax.broadcasted_iota(jnp.int32, (24, 80), 1) - ((row >> 2) & 3) * 20
-    pick = (pick == lax.broadcasted_iota(jnp.int32, (24, 80), 0)) & (pick < 20)
+    mixed[...] = sums.reshape(40, 8, 1024)
+    pick = lax.broadcasted_iota(jnp.int32, (40, 80), 1) - ((row >> 2) & 1) * 40
+    pick = pick == lax.broadcasted_iota(jnp.int32, (40, 80), 0)
     own = jnp.dot(pick.astype(F32).astype(BF), normed[:80, :], preferred_element_type=F32)
 
     def stacked(value):
-        return jnp.concatenate([value[:, g * 256 : (g + 1) * 256] for g in range(8)], axis=0).astype(BF)
+        return jnp.concatenate([value[:, g * 256 : (g + 1) * 256] for g in range(4)], axis=0).astype(BF)
 
     own = stacked(own)
     result = None
     for h in range(8):
-        value = jnp.dot(stacked(tall(mixed[:, h, :], 24)), value_weight[h], preferred_element_type=F32)
+        value = jnp.dot(stacked(mixed[:, h, :]), value_weight[h], preferred_element_type=F32)
         gate = jnp.dot(own, gate_weight[h], preferred_element_type=F32)
         gated = (jax.nn.sigmoid(gate) * value).astype(BF)
         term = jnp.dot(gated, final_weight[h], preferred_element_type=F32)
         result = term if result is None else result + term
-    for v, out in enumerate((out_a, out_b, out_c, out_d)):
-        out[...] = result[v * 48 : (v + 1) * 48]
+    out_a[...] = result[:80]
+    out_b[...] = result[80:]
 
 
 def average(parts, everyone, value_weight, gate_weight, final_weight):
     return call(
         average_body, 0, (1,),
-        [full((4, 160, 128))] * 4 + [full((4, 2, 4, 16, 2560))] * 2 + [
+        [full((4, 320, 128))] * 2 + [full((2, 320, 128))] * 2 + [full((4, 320, 128))] + [full((4, 2, 2, 16, 2560))] * 2 + [
             full((8, 256, 128)), full((8, 256, 128)), full((8, 128, 256))
         ],
-        [full((48, 256))] * 4, [shaped(F32, 48, 256)] * 4,
-        [pltpu.VMEM((16, 160, 128), F32), pltpu.VMEM((20, 8, 2048), F32), pltpu.VMEM((1280, 2048), BF)],
-        (3 * 10**9, 8 * 10**6, 10**5),
+        [full((80, 256))] * 2, [shaped(F32, 80, 256)] * 2,
+        [pltpu.VMEM((16, 320, 128), F32), pltpu.VMEM((40, 8, 1024), F32), pltpu.VMEM((1280, 1024), BF)],
+        (3 * 10**9, 8 * 10**6, 10**5), 36,
     )(*parts, *everyone, value_weight, gate_weight, final_weight)
 
 
-def epilogue_body(part_a, part_b, part_c, part_d, homolog, out, pieces):
-    row = lax.axis_index("row")
-    for v, part in enumerate((part_a, part_b, part_c, part_d)):
-        pieces[v] = part[...]
+def epilogue_body(part_a, part_b, homolog, out, pieces):
+    parity = (lax.axis_index("row") >> 2) & 1
+    pieces[0] = part_a[...]
+    pieces[1] = part_b[...]
     for half in range(2):
-        rows = jnp.concatenate(
-            [pieces[(q - (row >> 2)) & 3][half * 24 : half * 24 + 20] for q in range(4)], axis=0
-        )
+        rows = jnp.concatenate([pieces[parity ^ q][half * 40 : half * 40 + 40] for q in range(2)], axis=0)
         turned = jnp.transpose(tall(rows, 128))
         for s in range(4):
             fresh = homolog[half * 4 + s].astype(F32) + turned[s * 64 : (s + 1) * 64, :80]
@@ -301,8 +304,8 @@
 def epilogue(parts, homolog):
     return call(
         epilogue_body, 0, (1,),
-        [full((48, 256))] * 4 + [full((8, 64, 80))], full((8, 64, 80)), shaped(BF, 8, 64, 80),
-        [pltpu.VMEM((4, 48, 256), F32)],
+        [full((80, 256))] * 2 + [full((8, 64, 80))], full((8, 64, 80)), shaped(BF, 8, 64, 80),
+        [pltpu.VMEM((2, 80, 256), F32)],
         (10**6, 4 * 10**5, 0),
     )(*parts, homolog)
 
@@ -325,19 +328,7 @@
 
 
 def along_z(value, m):
-    return route(value, lambda z, x, y, h, c: ((z + m) % 4, x, y, h, c))
-
-
-def along_y(value, m):
-    return route(value, lambda z, x, y, h, c: (z, x, (y + m) % 4, h, c))
-
-
-def along_x(value, m):
-    return route(value, lambda z, x, y, h, c: (z, (x + m) % 4, y, h, c))
-
-
-def along_z(value, m):
-    return route(value, lambda z, x, y, h, c: ((z + m) % 4, x, y, h, c))
+    return route(value, lambda z, x, y, h, c: (z ^ m, x, y, h, c))
 
 
 def along_y(value, m):
@@ -386,7 +377,7 @@
     feedforward_shrink_matrix,
 ):
     homolog = jnp.swapaxes(homolog_matrix, 1, 2)
-    left, shared = prologue(seqs, residues, homolog, tensor_product_matrices[0])
+    left, right, shared = prologue(seqs, residues, homolog, tensor_product_matrices[0])
     product_weight, value_weight, gate_weight, mixing_weight = arrange_weights(
         tensor_product_final[0], mixing_value_gate_matrix[0], mixing_final_matrix[0].T
     )
@@ -394,13 +385,14 @@
     halves = jnp.stack([
         route(left, lambda z, x, y, h, c, u=u: (y, 2 * h + c, z, (x >> 1) ^ u, x & 1)) for u in range(2)
     ])
-    shared = jnp.stack([shared] + [along_z(shared, m) for m in (1, 2, 3)])
-    column = shared[:, 16:]
+    partner = along_z(shared, 1)
+    column = jnp.stack([right, partner[16:]] + [along_z(right, m) for m in (2, 3)])
     left_half = jnp.stack([halves] + [along_y(halves, m) for m in (1, 2, 3)])
     right = [column] + [along_x(column, m) for m in (1, 3, 2)]
     right[2], right[3] = right[3], right[2]
     left_all = [left_half, core_swap(left_half)]
-    group = after(shared[:, :16], *left_all, *right)
+    group = jnp.stack([shared[:16], partner[:16]])
+    group = after(group, *left_all, *right)
     group = jnp.stack([group, across(group)])
 
     contact, weights = outer(
@@ -411,16 +403,15 @@
     weights = route(weights, lambda z, x, y, h, c: (y, 2 * h + c, z, x >> 1, x & 1))
     pair = transition(contact, feedforward_gate_expand[0], feedforward_shrink_matrix[0])
     weights, behind, ahead, pair = lax.optimization_barrier((weights, behind, ahead, pair))
-    weights = jnp.stack([weights[0]] + [along_z(weights[v], v) for v in (1, 2, 3)])
+    weights = jnp.stack([weights[0]] + [along_z(weights[v & 1], v) for v in (1, 2, 3)])
     opposite = jnp.stack([along_y(behind[0], 1), along_y(ahead[1], 3)])
     weights, opposite = lax.optimization_barrier((weights, opposite))
-    weights = [weights] + [along_x(weights, m) for m in (1, 3, 2)]
-    weights[2], weights[3] = weights[3], weights[2]
+    after_x, before_x = along_x(weights, 1), along_x(weights, 3)
+    weights = [weights, after_x, along_x(after_x[:2], 1), along_x(before_x[2:], 3), before_x]
     everyone = jnp.stack([group, behind, opposite, ahead])
     everyone = [everyone, core_swap(everyone)]
-    own, *others = average(weights, everyone, value_weight, gate_weight, mixing_weight)
-    others = [along_z(part, 4 - v) for v, part in zip((1, 2, 3), others)]
-    msa = epilogue([own] + others, homolog)
+    own, other = average(weights, everyone, value_weight, gate_weight, mixing_weight)
+    msa = epilogue([own, along_z(other, 1)], homolog)
     return jnp.swapaxes(msa, 1, 2), pair
 
 

time: 130 us -> 124 us (0.954)
  waiting for transfers between devices: 32.2 us -> 24.6 us
  starting transfers between devices: 55.6 us -> 59.6 us
  local copies, waits for them, and re-layouts: 5.71 us -> 4.27 us
    ppermute x28 -> x27, waiting for transfers between devices: 32.2 us -> 24.6 us  [route(): return lax.ppermute(value, ('row', 'col'), pairs)]
    ppermute x28 -> x27, starting transfers between devices: 55.6 us -> 59.6 us  [route(): return lax.ppermute(value, ('row', 'col'), pairs)]
    unnamed x22 -> x20, local copies, waits for them, and re-layouts: 5.66 us -> 4.18 us
  transfers between devices with their start and end apart: 28 -> 27, of which waited for: 12 -> 8; matrix products, arithmetic and copies ran while one was open for 0% -> 0% of each run, Pallas kernels for 21% -> 22%
where the time goes in v3:
time: 124 us
  starting transfers between devices  59.6 us (48%)
  Pallas kernels  32.7 us (26%)
  waiting for transfers between devices  24.6 us (20%)
  local copies, waits for them, and re-layouts  4.27 us (3%)
  between operations  2.18 us (2%)
    ppermute x27, starting transfers between devices, route(): return lax.ppermute(value, ('row', 'col'), pairs)  59.6 us
    ppermute x27, waiting for transfers between devices, route(): return lax.ppermute(value, ('row', 'col'), pairs)  24.6 us
    pallas_call x1, Pallas kernels, outer(): call(outer_body, 2, (80 // ROWS,), [full((4, 2, 8, 2560))] * 2 + [full((4...  15.4 us
    pallas_call x1, Pallas kernels, transition(): call(transition_body, 0, (10,), [block, full((128, 1024)), full((512, 128...  10.7 us
    pallas_call x1, Pallas kernels, average(): call(average_body, 0, (1,), [full((4, 320, 128))] * 2 + [full((2, 320, 12...  4.41 us
    unnamed x20, local copies, waits for them, and re-layouts  4.18 us
  transfers between devices with their start and end apart: 27, of which 8 were waited for; matrix products, arithmetic and copies ran while one was open for 0% of the time, Pallas kernels for 22%

profile of v3, /device:TPU:1, one launch (start us, length us, event | category | flops | bytes accessed | tf_op | source)
XLA Modules:
  0.0 123.7 jit_solution(2724397527337637634)
XLA Ops:
  4.2 9.3 %collective-permute-start.1 = (bf16[8,2560]{1,0:T(8,128)(2,1)S(1)}, bf16[8,2560]{1,0:T(8,128)(2,1)S(1)}, u32[]{:S(2)}, u32[]{:S(2)}) collective-permute-start(bf16[8,2560]{1,0:T(8,128)(2,1)S(1)} %get-tuple-element.21), channel_id=1, source_target_pairs={{0,2},{1,18},{2,34},{3,50},{4,66},{5,82},{6,98},{7,114},{8,130},{9... | collective-permute-start | bytes 122888 | tf_op jit(solution)/shard_map/ppermute | solution.py:323
  13.5 1.9 %collective-permute-start = (bf16[8,2560]{1,0:T(8,128)(2,1)S(1)}, bf16[8,2560]{1,0:T(8,128)(2,1)S(1)}, u32[]{:S(2)}, u32[]{:S(2)}) collective-permute-start(bf16[8,2560]{1,0:T(8,128)(2,1)S(1)} %get-tuple-element.21), channel_id=1, source_target_pairs={{0,0},{1,16},{2,32},{3,48},{4,64},{5,80},{6,96},{7,112},{8,128},{9... | collective-permute-start | bytes 122888 | tf_op jit(solution)/shard_map/ppermute | solution.py:323
  15.4 3.8 %collective-permute-start.8 = (bf16[8,2560]{1,0:T(8,128)(2,1)S(1)}, bf16[8,2560]{1,0:T(8,128)(2,1)S(1)}, u32[]{:S(2)}, u32[]{:S(2)}) collective-permute-start(bf16[8,2560]{1,0:T(8,128)(2,1)S(1)} %get-tuple-element.22), channel_id=1, source_target_pairs={{0,192},{1,193},{2,194},{3,195},{4,196},{5,197},{6,198},{7,199},{8... | collective-permute-start | bytes 122888 | tf_op jit(solution)/shard_map/ppermute | solution.py:323
  23.0 4.8 %collective-permute-start.3 = (bf16[2,8,2560]{2,1,0:T(8,128)(2,1)S(1)}, bf16[2,8,2560]{2,1,0:T(8,128)(2,1)S(1)}, u32[]{:S(2)}, u32[]{:S(2)}) collective-permute-start(bf16[2,8,2560]{2,1,0:T(8,128)(2,1)S(1)} %get-tuple-element.44), channel_id=1, source_target_pairs={{0,8},{1,9},{2,10},{3,11},{4,12},{5,13},{6,14},{7,15},{8,0},{9,1},... | collective-permute-start | bytes 245768 | tf_op jit(solution)/shard_map/ppermute | solution.py:323
  27.9 2.6 %collective-permute-start.4 = (bf16[2,8,2560]{2,1,0:T(8,128)(2,1)S(1)}, bf16[2,8,2560]{2,1,0:T(8,128)(2,1)S(1)}, u32[]{:S(2)}, u32[]{:S(2)}) collective-permute-start(bf16[2,8,2560]{2,1,0:T(8,128)(2,1)S(1)} %get-tuple-element.44), channel_id=1, source_target_pairs={{0,12},{1,13},{2,14},{3,15},{4,0},{5,1},{6,2},{7,3},{8,4},{9,5},{1... | collective-permute-start | bytes 245768 | tf_op jit(solution)/shard_map/ppermute | solution.py:323
  30.6 3.8 %collective-permute-start.11 = (bf16[4,8,2560]{2,1,0:T(8,128)(2,1)S(1)}, bf16[4,8,2560]{2,1,0:T(8,128)(2,1)S(1)}, u32[]{:S(2)}, u32[]{:S(2)}) collective-permute-start(bf16[4,8,2560]{2,1,0:T(8,128)(2,1)S(1)} %pad_maximum_fusion.5.right_a), channel_id=1, source_target_pairs={{0,48},{1,49},{2,50},{3,51},{4,52},{5,53},{6,54},{7,55},{8,56},{9,... | collective-permute-start | bytes 491528 | tf_op jit(solution)/shard_map/ppermute | solution.py:323
  35.1 4.3 %collective-permute-start.5 = (bf16[4,2,8,2560]{3,2,1,0:T(8,128)(2,1)S(1)}, bf16[4,2,8,2560]{3,2,1,0:T(8,128)(2,1)S(1)}, u32[]{:S(2)}, u32[]{:S(2)}) collective-permute-start(bf16[4,2,8,2560]{3,2,1,0:T(8,128)(2,1)S(1)} %pad_maximum_fusion.1.left_a), channel_id=1, source_target_pairs={{0,1},{1,0},{2,3},{3,2},{4,5},{5,4},{6,7},{7,6},{8,9},{9,8},{10,11... | collective-permute-start | bytes 983048 | tf_op jit(solution)/shard_map/ppermute | solution.py:323
  40.1 1.7 %collective-permute-done.9.right_b = bf16[4,8,2560]{2,1,0:T(8,128)(2,1)S(1)} collective-permute-done((bf16[4,8,2560]{2,1,0:T(8,128)(2,1)S(1)}, bf16[4,8,2560]{2,1,0:T(8,128)(2,1)S(1)}, u32[]{:S(2)}, u32[]{:S(2)}) %collective-permute-start.9) | collective-permute-done | bytes 163872 | tf_op jit(solution)/shard_map/ppermute | solution.py:323
  41.9 15.4 %outer_body.1 = (bf16[80,80,128]{2,1,0:T(8,128)(2,1)S(1)}, bf16[2,320,128]{2,1,0:T(8,128)(2,1)S(1)}) custom-call(s32[1]{0:T(128)S(6)} %copy.13.seqs, s32[1]{0:T(128)S(6)} %copy.14.residues, bf16[4,2,8,2560]{3,2,1,0:T(8,128)(2,1)S(1)} %pad_maximum_fusion.1.left_a, bf16[4,2,8,2560]{3,2,1,0:T(8,128)(2,1)S(1)} %collective-permute-done.5.left_b, ...), custom_call_target="tpu_custom_call" | custom-call | flops 12000000000 | bytes 6000000 | tf_op jit(solution)/shard_map/outer_body/pallas_call | solution.py:189
  57.3 5.7 %collective-permute-start.12 = (bf16[2,320,128]{2,1,0:T(8,128)(2,1)S(1)}, bf16[2,320,128]{2,1,0:T(8,128)(2,1)S(1)}, u32[]{:S(2)}, u32[]{:S(2)}) collective-permute-start(bf16[2,320,128]{2,1,0:T(8,128)(2,1)S(1)} %get-tuple-element.25), channel_id=1, source_target_pairs={{0,0},{1,16},{2,32},{3,48},{4,64},{5,80},{6,96},{7,112},{8,128},{9... | collective-permute-start | bytes 491528 | tf_op jit(solution)/shard_map/ppermute | solution.py:323
  63.1 4.8 %collective-permute-start.15 = (bf16[2,2,16,2560]{3,2,1,0:T(8,128)(2,1)S(1)}, bf16[2,2,16,2560]{3,2,1,0:T(8,128)(2,1)S(1)}, u32[]{:S(2)}, u32[]{:S(2)}) collective-permute-start(bf16[2,2,16,2560]{3,2,1,0:T(8,128)(2,1)S(1)} %pad_maximum_fusion.2), channel_id=1, source_target_pairs={{0,12},{1,13},{2,14},{3,15},{4,0},{5,1},{6,2},{7,3},{8,4},{9,5},{1... | collective-permute-start | bytes 983048 | tf_op jit(solution)/shard_map/ppermute | solution.py:323
  67.9 10.7 %transition_body.1 = bf16[80,80,128]{2,1,0:T(8,128)(2,1)} custom-call(bf16[80,80,128]{2,1,0:T(8,128)(2,1)S(1)} %get-tuple-element.28.contact, bf16[128,1024]{1,0:T(8,128)(2,1)S(1)} %bitcast.54, bf16[512,128]{1,0:T(8,128)(2,1)S(1)} %bitcast.55), custom_call_target="tpu_custom_call" | custom-call | flops 5000000000 | bytes 3300000 | tf_op jit(solution)/shard_map/transition_body/pallas_call | solution.py:214
  78.6 2.2 %collective-permute-done.14 = bf16[2,2,16,2560]{3,2,1,0:T(8,128)(2,1)S(1)} collective-permute-done((bf16[2,2,16,2560]{3,2,1,0:T(8,128)(2,1)S(1)}, bf16[2,2,16,2560]{3,2,1,0:T(8,128)(2,1)S(1)}, u32[]{:S(2)}, u32[]{:S(2)}) %collective-permute-start.14) | collective-permute-done | bytes 327712 | tf_op jit(solution)/shard_map/ppermute | solution.py:323
  80.9 3.5 %collective-permute-start.16 = (bf16[320,128]{1,0:T(8,128)(2,1)S(1)}, bf16[320,128]{1,0:T(8,128)(2,1)S(1)}, u32[]{:S(2)}, u32[]{:S(2)}) collective-permute-start(bf16[320,128]{1,0:T(8,128)(2,1)S(1)} %get-tuple-element.42), channel_id=1, source_target_pairs={{0,64},{1,65},{2,66},{3,67},{4,68},{5,69},{6,70},{7,71},{8,72},{9,... | collective-permute-start | bytes 245768 | tf_op jit(solution)/shard_map/ppermute | solution.py:323
  85.0 1.8 %collective-permute-start.19 = (bf16[2,16,2560]{2,1,0:T(8,128)(2,1)S(1)}, bf16[2,16,2560]{2,1,0:T(8,128)(2,1)S(1)}, u32[]{:S(2)}, u32[]{:S(2)}) collective-permute-start(bf16[2,16,2560]{2,1,0:T(8,128)(2,1)S(1)} %slice_bitcast_fusion.1), channel_id=1, source_target_pairs={{0,4},{1,5},{2,6},{3,7},{4,8},{5,9},{6,10},{7,11},{8,12},{9,13},{1... | collective-permute-start | bytes 491528 | tf_op jit(solution)/shard_map/ppermute | solution.py:323
  86.8 3.8 %collective-permute-done.17 = bf16[320,128]{1,0:T(8,128)(2,1)S(1)} collective-permute-done((bf16[320,128]{1,0:T(8,128)(2,1)S(1)}, bf16[320,128]{1,0:T(8,128)(2,1)S(1)}, u32[]{:S(2)}, u32[]{:S(2)}) %collective-permute-start.17) | collective-permute-done | bytes 81952 | tf_op jit(solution)/shard_map/ppermute | solution.py:323
  90.9 4.9 %collective-permute-start.25 = (bf16[4,2,2,16,2560]{4,3,2,1,0:T(8,128)(2,1)S(1)}, bf16[4,2,2,16,2560]{4,3,2,1,0:T(8,128)(2,1)S(1)}, u32[]{:S(2)}, u32[]{:S(2)}) collective-permute-start(bf16[4,2,2,16,2560]{4,3,2,1,0:T(8,128)(2,1)S(1)} %pad_maximum_fusion.everyone_a), channel_id=1, source_target_pairs={{0,1},{1,0},{2,3},{3,2},{4,5},{5,4},{6,7},{7,6},{8,9},{9,8},{10,11... | collective-permute-start | bytes 3932168 | tf_op jit(solution)/shard_map/ppermute | solution.py:323
  95.8 2.7 %collective-permute-start.23 = (bf16[4,320,128]{2,1,0:T(8,128)(2,1)S(1)}, bf16[4,320,128]{2,1,0:T(8,128)(2,1)S(1)}, u32[]{:S(2)}, u32[]{:S(2)}) collective-permute-start(bf16[4,320,128]{2,1,0:T(8,128)(2,1)S(1)} %pad_maximum_fusion.3.part_a), channel_id=1, source_target_pairs={{0,48},{1,49},{2,50},{3,51},{4,52},{5,53},{6,54},{7,55},{8,56},{9,... | collective-permute-start | bytes 983048 | tf_op jit(solution)/shard_map/ppermute | solution.py:323
  98.5 7.1 %collective-permute-done.23.part_e = bf16[4,320,128]{2,1,0:T(8,128)(2,1)S(1)} collective-permute-done((bf16[4,320,128]{2,1,0:T(8,128)(2,1)S(1)}, bf16[4,320,128]{2,1,0:T(8,128)(2,1)S(1)}, u32[]{:S(2)}, u32[]{:S(2)}) %collective-permute-start.23) | collective-permute-done | bytes 327712 | tf_op jit(solution)/shard_map/ppermute | solution.py:323
  105.6 3.5 %collective-permute-start.24 = (bf16[2,320,128]{2,1,0:T(8,128)(2,1)S(1)}, bf16[2,320,128]{2,1,0:T(8,128)(2,1)S(1)}, u32[]{:S(2)}, u32[]{:S(2)}) collective-permute-start(bf16[2,320,128]{2,1,0:T(8,128)(2,1)S(1)} %slice.41), channel_id=1, source_target_pairs={{0,48},{1,49},{2,50},{3,51},{4,52},{5,53},{6,54},{7,55},{8,56},{9,... | collective-permute-start | bytes 491528 | tf_op jit(solution)/shard_map/ppermute | solution.py:323
  109.4 2.5 %collective-permute-done.24.part_d = bf16[2,320,128]{2,1,0:T(8,128)(2,1)S(1)} collective-permute-done((bf16[2,320,128]{2,1,0:T(8,128)(2,1)S(1)}, bf16[2,320,128]{2,1,0:T(8,128)(2,1)S(1)}, u32[]{:S(2)}, u32[]{:S(2)}) %collective-permute-start.24) | collective-permute-done | bytes 163872 | tf_op jit(solution)/shard_map/ppermute | solution.py:323
  111.8 3.3 %collective-permute-done.22.part_c = bf16[2,320,128]{2,1,0:T(8,128)(2,1)S(1)} collective-permute-done((bf16[2,320,128]{2,1,0:T(8,128)(2,1)S(1)}, bf16[2,320,128]{2,1,0:T(8,128)(2,1)S(1)}, u32[]{:S(2)}, u32[]{:S(2)}) %collective-permute-start.22) | collective-permute-done | bytes 163872 | tf_op jit(solution)/shard_map/ppermute | solution.py:323
  115.1 4.4 %average_body.1 = (f32[80,256]{1,0:T(8,128)S(1)}, f32[80,256]{1,0:T(8,128)S(1)}) custom-call(bf16[4,320,128]{2,1,0:T(8,128)(2,1)S(1)} %pad_maximum_fusion.3.part_a, bf16[4,320,128]{2,1,0:T(8,128)(2,1)S(1)} %collective-permute-done.21.part_b, bf16[2,320,128]{2,1,0:T(8,128)(2,1)S(1)} %collective-permute-done.22.part_c, ...), custom_call_target="tpu_custom_call" | custom-call | flops 3000000000 | bytes 8000000 | tf_op jit(solution)/shard_map/average_body/pallas_call | solution.py:281
  119.6 3.3 %collective-permute-done.26.part_b = f32[80,256]{1,0:T(8,128)S(1)} collective-permute-done((f32[80,256]{1,0:T(8,128)S(1)}, f32[80,256]{1,0:T(8,128)S(1)}, u32[]{:S(2)}, u32[]{:S(2)}) %collective-permute-start.26) | collective-permute-done | bytes 81952 | tf_op jit(solution)/shard_map/ppermute | solution.py:323
  (72 shorter events, 9.9 us)
Async XLA Ops:
  4.2 18.8 %collective-permute-start.1 = (bf16[8,2560]{1,0:T(8,128)(2,1)S(1)}, bf16[8,2560]{1,0:T(8,128)(2,1)S(1)}, u32[]{:S(2)}, u32[]{:S(2)}) collective-permute-start(bf16[8,2560]{1,0:T(8,128)(2,1)S(1)} %get-tuple-element.21), channel_id=1, source_target_pairs={{0,2},{1,18},{2,34},{3,50},{4,66},{5,82},{6,98},{7,114},{8,130},{9... | collective-permute-start | bytes 122888 | tf_op jit(solution)/shard_map/ppermute | solution.py:323
  13.5 9.5 %collective-permute-start = (bf16[8,2560]{1,0:T(8,128)(2,1)S(1)}, bf16[8,2560]{1,0:T(8,128)(2,1)S(1)}, u32[]{:S(2)}, u32[]{:S(2)}) collective-permute-start(bf16[8,2560]{1,0:T(8,128)(2,1)S(1)} %get-tuple-element.21), channel_id=1, source_target_pairs={{0,0},{1,16},{2,32},{3,48},{4,64},{5,80},{6,96},{7,112},{8,128},{9... | collective-permute-start | bytes 122888 | tf_op jit(solution)/shard_map/ppermute | solution.py:323
  15.4 15.1 %collective-permute-start.8 = (bf16[8,2560]{1,0:T(8,128)(2,1)S(1)}, bf16[8,2560]{1,0:T(8,128)(2,1)S(1)}, u32[]{:S(2)}, u32[]{:S(2)}) collective-permute-start(bf16[8,2560]{1,0:T(8,128)(2,1)S(1)} %get-tuple-element.22), channel_id=1, source_target_pairs={{0,192},{1,193},{2,194},{3,195},{4,196},{5,197},{6,198},{7,199},{8... | collective-permute-start | bytes 122888 | tf_op jit(solution)/shard_map/ppermute | solution.py:323
  19.2 11.3 %collective-permute-start.7 = (bf16[8,2560]{1,0:T(8,128)(2,1)S(1)}, bf16[8,2560]{1,0:T(8,128)(2,1)S(1)}, u32[]{:S(2)}, u32[]{:S(2)}) collective-permute-start(bf16[8,2560]{1,0:T(8,128)(2,1)S(1)} %get-tuple-element.22), channel_id=1, source_target_pairs={{0,128},{1,129},{2,130},{3,131},{4,132},{5,133},{6,134},{7,135},{8... | collective-permute-start | bytes 122888 | tf_op jit(solution)/shard_map/ppermute | solution.py:323
  19.2 8.8 %collective-permute-start.6 = (bf16[24,2560]{1,0:T(8,128)(2,1)S(1)}, bf16[24,2560]{1,0:T(8,128)(2,1)S(1)}, u32[]{:S(2)}, u32[]{:S(2)}) collective-permute-start(bf16[24,2560]{1,0:T(8,128)(2,1)S(1)} %get-tuple-element.23), channel_id=1, source_target_pairs={{0,64},{1,65},{2,66},{3,67},{4,68},{5,69},{6,70},{7,71},{8,72},{9,... | collective-permute-start | bytes 368648 | tf_op jit(solution)/shard_map/ppermute | solution.py:323
  23.0 11.3 %collective-permute-start.3 = (bf16[2,8,2560]{2,1,0:T(8,128)(2,1)S(1)}, bf16[2,8,2560]{2,1,0:T(8,128)(2,1)S(1)}, u32[]{:S(2)}, u32[]{:S(2)}) collective-permute-start(bf16[2,8,2560]{2,1,0:T(8,128)(2,1)S(1)} %get-tuple-element.44), channel_id=1, source_target_pairs={{0,8},{1,9},{2,10},{3,11},{4,12},{5,13},{6,14},{7,15},{8,0},{9,1},... | collective-permute-start | bytes 245768 | tf_op jit(solution)/shard_map/ppermute | solution.py:323
  27.8 7.2 %collective-permute-start.2 = (bf16[2,8,2560]{2,1,0:T(8,128)(2,1)S(1)}, bf16[2,8,2560]{2,1,0:T(8,128)(2,1)S(1)}, u32[]{:S(2)}, u32[]{:S(2)}) collective-permute-start(bf16[2,8,2560]{2,1,0:T(8,128)(2,1)S(1)} %get-tuple-element.44), channel_id=1, source_target_pairs={{0,4},{1,5},{2,6},{3,7},{4,8},{5,9},{6,10},{7,11},{8,12},{9,13},{1... | collective-permute-start | bytes 245768 | tf_op jit(solution)/shard_map/ppermute | solution.py:323
  27.9 7.1 %collective-permute-start.4 = (bf16[2,8,2560]{2,1,0:T(8,128)(2,1)S(1)}, bf16[2,8,2560]{2,1,0:T(8,128)(2,1)S(1)}, u32[]{:S(2)}, u32[]{:S(2)}) collective-permute-start(bf16[2,8,2560]{2,1,0:T(8,128)(2,1)S(1)} %get-tuple-element.44), channel_id=1, source_target_pairs={{0,12},{1,13},{2,14},{3,15},{4,0},{5,1},{6,2},{7,3},{8,4},{9,5},{1... | collective-permute-start | bytes 245768 | tf_op jit(solution)/shard_map/ppermute | solution.py:323
  30.6 8.8 %collective-permute-start.11 = (bf16[4,8,2560]{2,1,0:T(8,128)(2,1)S(1)}, bf16[4,8,2560]{2,1,0:T(8,128)(2,1)S(1)}, u32[]{:S(2)}, u32[]{:S(2)}) collective-permute-start(bf16[4,8,2560]{2,1,0:T(8,128)(2,1)S(1)} %pad_maximum_fusion.5.right_a), channel_id=1, source_target_pairs={{0,48},{1,49},{2,50},{3,51},{4,52},{5,53},{6,54},{7,55},{8,56},{9,... | collective-permute-start | bytes 491528 | tf_op jit(solution)/shard_map/ppermute | solution.py:323
  34.3 7.5 %collective-permute-start.9 = (bf16[4,8,2560]{2,1,0:T(8,128)(2,1)S(1)}, bf16[4,8,2560]{2,1,0:T(8,128)(2,1)S(1)}, u32[]{:S(2)}, u32[]{:S(2)}) collective-permute-start(bf16[4,8,2560]{2,1,0:T(8,128)(2,1)S(1)} %pad_maximum_fusion.5.right_a), channel_id=1, source_target_pairs={{0,16},{1,17},{2,18},{3,19},{4,20},{5,21},{6,22},{7,23},{8,24},{9,... | collective-permute-start | bytes 491528 | tf_op jit(solution)/shard_map/ppermute | solution.py:323
  35.1 6.8 %collective-permute-start.5 = (bf16[4,2,8,2560]{3,2,1,0:T(8,128)(2,1)S(1)}, bf16[4,2,8,2560]{3,2,1,0:T(8,128)(2,1)S(1)}, u32[]{:S(2)}, u32[]{:S(2)}) collective-permute-start(bf16[4,2,8,2560]{3,2,1,0:T(8,128)(2,1)S(1)} %pad_maximum_fusion.1.left_a), channel_id=1, source_target_pairs={{0,1},{1,0},{2,3},{3,2},{4,5},{5,4},{6,7},{7,6},{8,9},{9,8},{10,11... | collective-permute-start | bytes 983048 | tf_op jit(solution)/shard_map/ppermute | solution.py:323
  41.9 21.2 %collective-permute-start.13 = (bf16[2,16,2560]{2,1,0:T(8,128)(2,1)S(1)}, bf16[2,16,2560]{2,1,0:T(8,128)(2,1)S(1)}, u32[]{:S(2)}, u32[]{:S(2)}) collective-permute-start(bf16[2,16,2560]{2,1,0:T(8,128)(2,1)S(1)} %pad_maximum_fusion.6), channel_id=1, source_target_pairs={{0,2},{1,3},{2,0},{3,1},{4,6},{5,7},{6,4},{7,5},{8,10},{9,11},{10,... | collective-permute-start | bytes 491528 | tf_op jit(solution)/shard_map/ppermute | solution.py:323
  57.3 21.2 %collective-permute-start.12 = (bf16[2,320,128]{2,1,0:T(8,128)(2,1)S(1)}, bf16[2,320,128]{2,1,0:T(8,128)(2,1)S(1)}, u32[]{:S(2)}, u32[]{:S(2)}) collective-permute-start(bf16[2,320,128]{2,1,0:T(8,128)(2,1)S(1)} %get-tuple-element.25), channel_id=1, source_target_pairs={{0,0},{1,16},{2,32},{3,48},{4,64},{5,80},{6,96},{7,112},{8,128},{9... | collective-permute-start | bytes 491528 | tf_op jit(solution)/shard_map/ppermute | solution.py:323
  63.1 15.5 %collective-permute-start.15 = (bf16[2,2,16,2560]{3,2,1,0:T(8,128)(2,1)S(1)}, bf16[2,2,16,2560]{3,2,1,0:T(8,128)(2,1)S(1)}, u32[]{:S(2)}, u32[]{:S(2)}) collective-permute-start(bf16[2,2,16,2560]{3,2,1,0:T(8,128)(2,1)S(1)} %pad_maximum_fusion.2), channel_id=1, source_target_pairs={{0,12},{1,13},{2,14},{3,15},{4,0},{5,1},{6,2},{7,3},{8,4},{9,5},{1... | collective-permute-start | bytes 983048 | tf_op jit(solution)/shard_map/ppermute | solution.py:323
  67.9 12.9 %collective-permute-start.14 = (bf16[2,2,16,2560]{3,2,1,0:T(8,128)(2,1)S(1)}, bf16[2,2,16,2560]{3,2,1,0:T(8,128)(2,1)S(1)}, u32[]{:S(2)}, u32[]{:S(2)}) collective-permute-start(bf16[2,2,16,2560]{3,2,1,0:T(8,128)(2,1)S(1)} %pad_maximum_fusion.2), channel_id=1, source_target_pairs={{0,4},{1,5},{2,6},{3,7},{4,8},{5,9},{6,10},{7,11},{8,12},{9,13},{1... | collective-permute-start | bytes 983048 | tf_op jit(solution)/shard_map/ppermute | solution.py:323
  80.8 9.8 %collective-permute-start.18 = (bf16[320,128]{1,0:T(8,128)(2,1)S(1)}, bf16[320,128]{1,0:T(8,128)(2,1)S(1)}, u32[]{:S(2)}, u32[]{:S(2)}) collective-permute-start(bf16[320,128]{1,0:T(8,128)(2,1)S(1)} %get-tuple-element.42), channel_id=1, source_target_pairs={{0,192},{1,193},{2,194},{3,195},{4,196},{5,197},{6,198},{7,199},{8... | collective-permute-start | bytes 245768 | tf_op jit(solution)/shard_map/ppermute | solution.py:323
  80.9 9.7 %collective-permute-start.16 = (bf16[320,128]{1,0:T(8,128)(2,1)S(1)}, bf16[320,128]{1,0:T(8,128)(2,1)S(1)}, u32[]{:S(2)}, u32[]{:S(2)}) collective-permute-start(bf16[320,128]{1,0:T(8,128)(2,1)S(1)} %get-tuple-element.42), channel_id=1, source_target_pairs={{0,64},{1,65},{2,66},{3,67},{4,68},{5,69},{6,70},{7,71},{8,72},{9,... | collective-permute-start | bytes 245768 | tf_op jit(solution)/shard_map/ppermute | solution.py:323
  84.4 6.2 %collective-permute-start.17 = (bf16[320,128]{1,0:T(8,128)(2,1)S(1)}, bf16[320,128]{1,0:T(8,128)(2,1)S(1)}, u32[]{:S(2)}, u32[]{:S(2)}) collective-permute-start(bf16[320,128]{1,0:T(8,128)(2,1)S(1)} %get-tuple-element.41), channel_id=1, source_target_pairs={{0,128},{1,129},{2,130},{3,131},{4,132},{5,133},{6,134},{7,135},{8... | collective-permute-start | bytes 245768 | tf_op jit(solution)/shard_map/ppermute | solution.py:323
  84.5 6.2 %collective-permute-start.20 = (bf16[2,16,2560]{2,1,0:T(8,128)(2,1)S(1)}, bf16[2,16,2560]{2,1,0:T(8,128)(2,1)S(1)}, u32[]{:S(2)}, u32[]{:S(2)}) collective-permute-start(bf16[2,16,2560]{2,1,0:T(8,128)(2,1)S(1)} %slice_bitcast_fusion), channel_id=1, source_target_pairs={{0,12},{1,13},{2,14},{3,15},{4,0},{5,1},{6,2},{7,3},{8,4},{9,5},{1... | collective-permute-start | bytes 491528 | tf_op jit(solution)/shard_map/ppermute | solution.py:323
  90.9 24.2 %collective-permute-start.25 = (bf16[4,2,2,16,2560]{4,3,2,1,0:T(8,128)(2,1)S(1)}, bf16[4,2,2,16,2560]{4,3,2,1,0:T(8,128)(2,1)S(1)}, u32[]{:S(2)}, u32[]{:S(2)}) collective-permute-start(bf16[4,2,2,16,2560]{4,3,2,1,0:T(8,128)(2,1)S(1)} %pad_maximum_fusion.everyone_a), channel_id=1, source_target_pairs={{0,1},{1,0},{2,3},{3,2},{4,5},{5,4},{6,7},{7,6},{8,9},{9,8},{10,11... | collective-permute-start | bytes 3932168 | tf_op jit(solution)/shard_map/ppermute | solution.py:323
  95.8 9.7 %collective-permute-start.23 = (bf16[4,320,128]{2,1,0:T(8,128)(2,1)S(1)}, bf16[4,320,128]{2,1,0:T(8,128)(2,1)S(1)}, u32[]{:S(2)}, u32[]{:S(2)}) collective-permute-start(bf16[4,320,128]{2,1,0:T(8,128)(2,1)S(1)} %pad_maximum_fusion.3.part_a), channel_id=1, source_target_pairs={{0,48},{1,49},{2,50},{3,51},{4,52},{5,53},{6,54},{7,55},{8,56},{9,... | collective-permute-start | bytes 983048 | tf_op jit(solution)/shard_map/ppermute | solution.py:323
  98.5 10.6 %collective-permute-start.21 = (bf16[4,320,128]{2,1,0:T(8,128)(2,1)S(1)}, bf16[4,320,128]{2,1,0:T(8,128)(2,1)S(1)}, u32[]{:S(2)}, u32[]{:S(2)}) collective-permute-start(bf16[4,320,128]{2,1,0:T(8,128)(2,1)S(1)} %pad_maximum_fusion.3.part_a), channel_id=1, source_target_pairs={{0,16},{1,17},{2,18},{3,19},{4,20},{5,21},{6,22},{7,23},{8,24},{9,... | collective-permute-start | bytes 983048 | tf_op jit(solution)/shard_map/ppermute | solution.py:323
  105.6 6.3 %collective-permute-start.24 = (bf16[2,320,128]{2,1,0:T(8,128)(2,1)S(1)}, bf16[2,320,128]{2,1,0:T(8,128)(2,1)S(1)}, u32[]{:S(2)}, u32[]{:S(2)}) collective-permute-start(bf16[2,320,128]{2,1,0:T(8,128)(2,1)S(1)} %slice.41), channel_id=1, source_target_pairs={{0,48},{1,49},{2,50},{3,51},{4,52},{5,53},{6,54},{7,55},{8,56},{9,... | collective-permute-start | bytes 491528 | tf_op jit(solution)/shard_map/ppermute | solution.py:323
  109.1 6.1 %collective-permute-start.22 = (bf16[2,320,128]{2,1,0:T(8,128)(2,1)S(1)}, bf16[2,320,128]{2,1,0:T(8,128)(2,1)S(1)}, u32[]{:S(2)}, u32[]{:S(2)}) collective-permute-start(bf16[2,320,128]{2,1,0:T(8,128)(2,1)S(1)} %slice.40), channel_id=1, source_target_pairs={{0,16},{1,17},{2,18},{3,19},{4,20},{5,21},{6,22},{7,23},{8,24},{9,... | collective-permute-start | bytes 491528 | tf_op jit(solution)/shard_map/ppermute | solution.py:323
  (13 other events, 136.9 us)

commit v4 on v3

--- a/solution.py
+++ b/solution.py
@@ -378,9 +378,6 @@
 ):
     homolog = jnp.swapaxes(homolog_matrix, 1, 2)
     left, right, shared = prologue(seqs, residues, homolog, tensor_product_matrices[0])
-    product_weight, value_weight, gate_weight, mixing_weight = arrange_weights(
-        tensor_product_final[0], mixing_value_gate_matrix[0], mixing_final_matrix[0].T
-    )
 
     halves = jnp.stack([
         route(left, lambda z, x, y, h, c, u=u: (y, 2 * h + c, z, (x >> 1) ^ u, x & 1)) for u in range(2)
@@ -391,8 +388,11 @@
     right = [column] + [along_x(column, m) for m in (1, 3, 2)]
     right[2], right[3] = right[3], right[2]
     left_all = [left_half, core_swap(left_half)]
+    product_weight, value_weight, gate_weight, mixing_weight = arrange_weights(
+        after(tensor_product_final[0], left_half), mixing_value_gate_matrix[0], mixing_final_matrix[0].T
+    )
     group = jnp.stack([shared[:16], partner[:16]])
-    group = after(group, *left_all, *right)
+    group = after(group, right[3])
     group = jnp.stack([group, across(group)])
 
     contact, weights = outer(

time: 124 us -> 123 us (level)
  starting transfers between devices: 59.6 us -> 63.7 us
  waiting for transfers between devices: 24.6 us -> 21 us
  local copies, waits for them, and re-layouts: 4.27 us -> 1.74 us
    ppermute x27, starting transfers between devices: 59.6 us -> 63.7 us  [route(): return lax.ppermute(value, ('row', 'col'), pairs)]
    ppermute x27, waiting for transfers between devices: 24.6 us -> 21 us  [route(): return lax.ppermute(value, ('row', 'col'), pairs)]
    unnamed x20, local copies, waits for them, and re-layouts: 4.18 us -> 1.65 us
  transfers between devices with their start and end apart: 27 -> 27, of which waited for: 8 -> 7; matrix products, arithmetic and copies ran while one was open for 0% -> 0% of each run, Pallas kernels for 22% -> 22%
where the time goes in v4:
time: 123 us; the launch traced here: 122 us
  starting transfers between devices  63.7 us (52%)
  Pallas kernels  32.7 us (27%)
  waiting for transfers between devices  21 us (17%)
  between operations  2.23 us (2%)
  local copies, waits for them, and re-layouts  1.74 us (1%)
    ppermute x27, starting transfers between devices, route(): return lax.ppermute(value, ('row', 'col'), pairs)  63.7 us
    ppermute x27, waiting for transfers between devices, route(): return lax.ppermute(value, ('row', 'col'), pairs)  21 us
    pallas_call x1, Pallas kernels, outer(): call(outer_body, 2, (80 // ROWS,), [full((4, 2, 8, 2560))] * 2 + [full((4...  15.4 us
    pallas_call x1, Pallas kernels, transition(): call(transition_body, 0, (10,), [block, full((128, 1024)), full((512, 128...  10.6 us
    pallas_call x1, Pallas kernels, average(): call(average_body, 0, (1,), [full((4, 320, 128))] * 2 + [full((2, 320, 12...  4.41 us
  transfers between devices with their start and end apart: 27, of which 7 were waited for; matrix products, arithmetic and copies ran while one was open for 0% of the time, Pallas kernels for 22%

profile of v4, /device:TPU:1, one launch (start us, length us, event | category | flops | bytes accessed | tf_op | source)
XLA Modules:
  0.0 121.7 jit_solution(11683507214057471521)
XLA Ops:
  4.2 9.3 %collective-permute-start.1 = (bf16[8,2560]{1,0:T(8,128)(2,1)S(1)}, bf16[8,2560]{1,0:T(8,128)(2,1)S(1)}, u32[]{:S(2)}, u32[]{:S(2)}) collective-permute-start(bf16[8,2560]{1,0:T(8,128)(2,1)S(1)} %get-tuple-element.22), channel_id=1, source_target_pairs={{0,2},{1,18},{2,34},{3,50},{4,66},{5,82},{6,98},{7,114},{8,130},{9... | collective-permute-start | bytes 122888 | tf_op jit(solution)/shard_map/ppermute | solution.py:323
  13.5 1.9 %collective-permute-start = (bf16[8,2560]{1,0:T(8,128)(2,1)S(1)}, bf16[8,2560]{1,0:T(8,128)(2,1)S(1)}, u32[]{:S(2)}, u32[]{:S(2)}) collective-permute-start(bf16[8,2560]{1,0:T(8,128)(2,1)S(1)} %get-tuple-element.22), channel_id=1, source_target_pairs={{0,0},{1,16},{2,32},{3,48},{4,64},{5,80},{6,96},{7,112},{8,128},{9... | collective-permute-start | bytes 122888 | tf_op jit(solution)/shard_map/ppermute | solution.py:323
  15.4 3.8 %collective-permute-start.8 = (bf16[8,2560]{1,0:T(8,128)(2,1)S(1)}, bf16[8,2560]{1,0:T(8,128)(2,1)S(1)}, u32[]{:S(2)}, u32[]{:S(2)}) collective-permute-start(bf16[8,2560]{1,0:T(8,128)(2,1)S(1)} %get-tuple-element.23), channel_id=1, source_target_pairs={{0,192},{1,193},{2,194},{3,195},{4,196},{5,197},{6,198},{7,199},{8... | collective-permute-start | bytes 122888 | tf_op jit(solution)/shard_map/ppermute | solution.py:323
  19.7 6.8 %collective-permute-start.3 = (bf16[2,8,2560]{2,1,0:T(8,128)(2,1)S(1)}, bf16[2,8,2560]{2,1,0:T(8,128)(2,1)S(1)}, u32[]{:S(2)}, u32[]{:S(2)}) collective-permute-start(bf16[2,8,2560]{2,1,0:T(8,128)(2,1)S(1)} %get-tuple-element.46), channel_id=1, source_target_pairs={{0,8},{1,9},{2,10},{3,11},{4,12},{5,13},{6,14},{7,15},{8,0},{9,1},... | collective-permute-start | bytes 245768 | tf_op jit(solution)/shard_map/ppermute | solution.py:323
  26.5 2.7 %collective-permute-start.4 = (bf16[2,8,2560]{2,1,0:T(8,128)(2,1)S(1)}, bf16[2,8,2560]{2,1,0:T(8,128)(2,1)S(1)}, u32[]{:S(2)}, u32[]{:S(2)}) collective-permute-start(bf16[2,8,2560]{2,1,0:T(8,128)(2,1)S(1)} %get-tuple-element.46), channel_id=1, source_target_pairs={{0,12},{1,13},{2,14},{3,15},{4,0},{5,1},{6,2},{7,3},{8,4},{9,5},{1... | collective-permute-start | bytes 245768 | tf_op jit(solution)/shard_map/ppermute | solution.py:323
  29.2 2.4 %collective-permute-start.11 = (bf16[4,8,2560]{2,1,0:T(8,128)(2,1)S(1)}, bf16[4,8,2560]{2,1,0:T(8,128)(2,1)S(1)}, u32[]{:S(2)}, u32[]{:S(2)}) collective-permute-start(bf16[4,8,2560]{2,1,0:T(8,128)(2,1)S(1)} %pad_maximum_fusion.5.right_a), channel_id=1, source_target_pairs={{0,48},{1,49},{2,50},{3,51},{4,52},{5,53},{6,54},{7,55},{8,56},{9,... | collective-permute-start | bytes 491528 | tf_op jit(solution)/shard_map/ppermute | solution.py:323
  32.4 3.6 %collective-permute-start.5 = (bf16[4,2,8,2560]{3,2,1,0:T(8,128)(2,1)S(1)}, bf16[4,2,8,2560]{3,2,1,0:T(8,128)(2,1)S(1)}, u32[]{:S(2)}, u32[]{:S(2)}) collective-permute-start(bf16[4,2,8,2560]{3,2,1,0:T(8,128)(2,1)S(1)} %pad_maximum_fusion.1.left_a), channel_id=1, source_target_pairs={{0,1},{1,0},{2,3},{3,2},{4,5},{5,4},{6,7},{7,6},{8,9},{9,8},{10,11... | collective-permute-start | bytes 983048 | tf_op jit(solution)/shard_map/ppermute | solution.py:323
  37.0 3.7 %collective-permute-start.13 = (bf16[2,16,2560]{2,1,0:T(8,128)(2,1)S(1)}, bf16[2,16,2560]{2,1,0:T(8,128)(2,1)S(1)}, u32[]{:S(2)}, u32[]{:S(2)}) collective-permute-start(bf16[2,16,2560]{2,1,0:T(8,128)(2,1)S(1)} %pad_maximum_fusion.6), channel_id=1, source_target_pairs={{0,2},{1,3},{2,0},{3,1},{4,6},{5,7},{6,4},{7,5},{8,10},{9,11},{10,... | collective-permute-start | bytes 491528 | tf_op jit(solution)/shard_map/ppermute | solution.py:323
  40.8 15.4 %outer_body.1 = (bf16[80,80,128]{2,1,0:T(8,128)(2,1)S(1)}, bf16[2,320,128]{2,1,0:T(8,128)(2,1)S(1)}) custom-call(s32[1]{0:T(128)S(6)} %copy.13.seqs, s32[1]{0:T(128)S(6)} %copy.14.residues, bf16[4,2,8,2560]{3,2,1,0:T(8,128)(2,1)S(1)} %pad_maximum_fusion.1.left_a, bf16[4,2,8,2560]{3,2,1,0:T(8,128)(2,1)S(1)} %collective-permute-done.5.left_b, ...), custom_call_target="tpu_custom_call" | custom-call | flops 12000000000 | bytes 6000000 | tf_op jit(solution)/shard_map/outer_body/pallas_call | solution.py:189
  56.2 3.0 %collective-permute-start.12 = (bf16[2,320,128]{2,1,0:T(8,128)(2,1)S(1)}, bf16[2,320,128]{2,1,0:T(8,128)(2,1)S(1)}, u32[]{:S(2)}, u32[]{:S(2)}) collective-permute-start(bf16[2,320,128]{2,1,0:T(8,128)(2,1)S(1)} %get-tuple-element.27), channel_id=1, source_target_pairs={{0,0},{1,16},{2,32},{3,48},{4,64},{5,80},{6,96},{7,112},{8,128},{9... | collective-permute-start | bytes 491528 | tf_op jit(solution)/shard_map/ppermute | solution.py:323
  59.3 4.4 %collective-permute-start.15 = (bf16[2,2,16,2560]{3,2,1,0:T(8,128)(2,1)S(1)}, bf16[2,2,16,2560]{3,2,1,0:T(8,128)(2,1)S(1)}, u32[]{:S(2)}, u32[]{:S(2)}) collective-permute-start(bf16[2,2,16,2560]{3,2,1,0:T(8,128)(2,1)S(1)} %pad_maximum_fusion.2), channel_id=1, source_target_pairs={{0,12},{1,13},{2,14},{3,15},{4,0},{5,1},{6,2},{7,3},{8,4},{9,5},{1... | collective-permute-start | bytes 983048 | tf_op jit(solution)/shard_map/ppermute | solution.py:323
  63.7 10.6 %transition_body.1 = bf16[80,80,128]{2,1,0:T(8,128)(2,1)} custom-call(bf16[80,80,128]{2,1,0:T(8,128)(2,1)S(1)} %get-tuple-element.30.contact, bf16[128,1024]{1,0:T(8,128)(2,1)S(1)} %bitcast.54, bf16[512,128]{1,0:T(8,128)(2,1)S(1)} %bitcast.55), custom_call_target="tpu_custom_call" | custom-call | flops 5000000000 | bytes 3300000 | tf_op jit(solution)/shard_map/transition_body/pallas_call | solution.py:214
  74.4 2.6 %collective-permute-done.14 = bf16[2,2,16,2560]{3,2,1,0:T(8,128)(2,1)S(1)} collective-permute-done((bf16[2,2,16,2560]{3,2,1,0:T(8,128)(2,1)S(1)}, bf16[2,2,16,2560]{3,2,1,0:T(8,128)(2,1)S(1)}, u32[]{:S(2)}, u32[]{:S(2)}) %collective-permute-start.14) | collective-permute-done | bytes 327712 | tf_op jit(solution)/shard_map/ppermute | solution.py:323
  77.1 6.8 %collective-permute-start.16 = (bf16[320,128]{1,0:T(8,128)(2,1)S(1)}, bf16[320,128]{1,0:T(8,128)(2,1)S(1)}, u32[]{:S(2)}, u32[]{:S(2)}) collective-permute-start(bf16[320,128]{1,0:T(8,128)(2,1)S(1)} %get-tuple-element.44), channel_id=1, source_target_pairs={{0,64},{1,65},{2,66},{3,67},{4,68},{5,69},{6,70},{7,71},{8,72},{9,... | collective-permute-start | bytes 245768 | tf_op jit(solution)/shard_map/ppermute | solution.py:323
  84.6 2.8 %collective-permute-start.19 = (bf16[2,16,2560]{2,1,0:T(8,128)(2,1)S(1)}, bf16[2,16,2560]{2,1,0:T(8,128)(2,1)S(1)}, u32[]{:S(2)}, u32[]{:S(2)}) collective-permute-start(bf16[2,16,2560]{2,1,0:T(8,128)(2,1)S(1)} %slice_bitcast_fusion.1), channel_id=1, source_target_pairs={{0,4},{1,5},{2,6},{3,7},{4,8},{5,9},{6,10},{7,11},{8,12},{9,13},{1... | collective-permute-start | bytes 491528 | tf_op jit(solution)/shard_map/ppermute | solution.py:323
  87.3 3.5 %collective-permute-done.17 = bf16[320,128]{1,0:T(8,128)(2,1)S(1)} collective-permute-done((bf16[320,128]{1,0:T(8,128)(2,1)S(1)}, bf16[320,128]{1,0:T(8,128)(2,1)S(1)}, u32[]{:S(2)}, u32[]{:S(2)}) %collective-permute-start.17) | collective-permute-done | bytes 81952 | tf_op jit(solution)/shard_map/ppermute | solution.py:323
  91.1 1.6 %collective-permute-start.25 = (bf16[4,2,2,16,2560]{4,3,2,1,0:T(8,128)(2,1)S(1)}, bf16[4,2,2,16,2560]{4,3,2,1,0:T(8,128)(2,1)S(1)}, u32[]{:S(2)}, u32[]{:S(2)}) collective-permute-start(bf16[4,2,2,16,2560]{4,3,2,1,0:T(8,128)(2,1)S(1)} %pad_maximum_fusion.everyone_a), channel_id=1, source_target_pairs={{0,1},{1,0},{2,3},{3,2},{4,5},{5,4},{6,7},{7,6},{8,9},{9,8},{10,11... | collective-permute-start | bytes 3932168 | tf_op jit(solution)/shard_map/ppermute | solution.py:323
  92.7 3.7 %collective-permute-start.23 = (bf16[4,320,128]{2,1,0:T(8,128)(2,1)S(1)}, bf16[4,320,128]{2,1,0:T(8,128)(2,1)S(1)}, u32[]{:S(2)}, u32[]{:S(2)}) collective-permute-start(bf16[4,320,128]{2,1,0:T(8,128)(2,1)S(1)} %pad_maximum_fusion.3.part_a), channel_id=1, source_target_pairs={{0,48},{1,49},{2,50},{3,51},{4,52},{5,53},{6,54},{7,55},{8,56},{9,... | collective-permute-start | bytes 983048 | tf_op jit(solution)/shard_map/ppermute | solution.py:323
  96.4 7.1 %collective-permute-done.23.part_e = bf16[4,320,128]{2,1,0:T(8,128)(2,1)S(1)} collective-permute-done((bf16[4,320,128]{2,1,0:T(8,128)(2,1)S(1)}, bf16[4,320,128]{2,1,0:T(8,128)(2,1)S(1)}, u32[]{:S(2)}, u32[]{:S(2)}) %collective-permute-start.23) | collective-permute-done | bytes 327712 | tf_op jit(solution)/shard_map/ppermute | solution.py:323
  103.5 3.5 %collective-permute-start.24 = (bf16[2,320,128]{2,1,0:T(8,128)(2,1)S(1)}, bf16[2,320,128]{2,1,0:T(8,128)(2,1)S(1)}, u32[]{:S(2)}, u32[]{:S(2)}) collective-permute-start(bf16[2,320,128]{2,1,0:T(8,128)(2,1)S(1)} %slice.41), channel_id=1, source_target_pairs={{0,48},{1,49},{2,50},{3,51},{4,52},{5,53},{6,54},{7,55},{8,56},{9,... | collective-permute-start | bytes 491528 | tf_op jit(solution)/shard_map/ppermute | solution.py:323
  107.3 2.3 %collective-permute-done.24.part_d = bf16[2,320,128]{2,1,0:T(8,128)(2,1)S(1)} collective-permute-done((bf16[2,320,128]{2,1,0:T(8,128)(2,1)S(1)}, bf16[2,320,128]{2,1,0:T(8,128)(2,1)S(1)}, u32[]{:S(2)}, u32[]{:S(2)}) %collective-permute-start.24) | collective-permute-done | bytes 163872 | tf_op jit(solution)/shard_map/ppermute | solution.py:323
  109.6 3.4 %collective-permute-done.22.part_c = bf16[2,320,128]{2,1,0:T(8,128)(2,1)S(1)} collective-permute-done((bf16[2,320,128]{2,1,0:T(8,128)(2,1)S(1)}, bf16[2,320,128]{2,1,0:T(8,128)(2,1)S(1)}, u32[]{:S(2)}, u32[]{:S(2)}) %collective-permute-start.22) | collective-permute-done | bytes 163872 | tf_op jit(solution)/shard_map/ppermute | solution.py:323
  113.1 4.4 %average_body.1 = (f32[80,256]{1,0:T(8,128)S(1)}, f32[80,256]{1,0:T(8,128)S(1)}) custom-call(bf16[4,320,128]{2,1,0:T(8,128)(2,1)S(1)} %pad_maximum_fusion.3.part_a, bf16[4,320,128]{2,1,0:T(8,128)(2,1)S(1)} %collective-permute-done.21.part_b, bf16[2,320,128]{2,1,0:T(8,128)(2,1)S(1)} %collective-permute-done.22.part_c, ...), custom_call_target="tpu_custom_call" | custom-call | flops 3000000000 | bytes 8000000 | tf_op jit(solution)/shard_map/average_body/pallas_call | solution.py:281
  119.0 1.9 %collective-permute-done.26.part_b = f32[80,256]{1,0:T(8,128)S(1)} collective-permute-done((f32[80,256]{1,0:T(8,128)S(1)}, f32[80,256]{1,0:T(8,128)S(1)}, u32[]{:S(2)}, u32[]{:S(2)}) %collective-permute-start.26) | collective-permute-done | bytes 81952 | tf_op jit(solution)/shard_map/ppermute | solution.py:323
  (72 shorter events, 8.2 us)
Async XLA Ops:
  4.2 15.4 %collective-permute-start.1 = (bf16[8,2560]{1,0:T(8,128)(2,1)S(1)}, bf16[8,2560]{1,0:T(8,128)(2,1)S(1)}, u32[]{:S(2)}, u32[]{:S(2)}) collective-permute-start(bf16[8,2560]{1,0:T(8,128)(2,1)S(1)} %get-tuple-element.22), channel_id=1, source_target_pairs={{0,2},{1,18},{2,34},{3,50},{4,66},{5,82},{6,98},{7,114},{8,130},{9... | collective-permute-start | bytes 122888 | tf_op jit(solution)/shard_map/ppermute | solution.py:323
  13.5 6.1 %collective-permute-start = (bf16[8,2560]{1,0:T(8,128)(2,1)S(1)}, bf16[8,2560]{1,0:T(8,128)(2,1)S(1)}, u32[]{:S(2)}, u32[]{:S(2)}) collective-permute-start(bf16[8,2560]{1,0:T(8,128)(2,1)S(1)} %get-tuple-element.22), channel_id=1, source_target_pairs={{0,0},{1,16},{2,32},{3,48},{4,64},{5,80},{6,96},{7,112},{8,128},{9... | collective-permute-start | bytes 122888 | tf_op jit(solution)/shard_map/ppermute | solution.py:323
  15.4 13.7 %collective-permute-start.8 = (bf16[8,2560]{1,0:T(8,128)(2,1)S(1)}, bf16[8,2560]{1,0:T(8,128)(2,1)S(1)}, u32[]{:S(2)}, u32[]{:S(2)}) collective-permute-start(bf16[8,2560]{1,0:T(8,128)(2,1)S(1)} %get-tuple-element.23), channel_id=1, source_target_pairs={{0,192},{1,193},{2,194},{3,195},{4,196},{5,197},{6,198},{7,199},{8... | collective-permute-start | bytes 122888 | tf_op jit(solution)/shard_map/ppermute | solution.py:323
  19.2 9.9 %collective-permute-start.7 = (bf16[8,2560]{1,0:T(8,128)(2,1)S(1)}, bf16[8,2560]{1,0:T(8,128)(2,1)S(1)}, u32[]{:S(2)}, u32[]{:S(2)}) collective-permute-start(bf16[8,2560]{1,0:T(8,128)(2,1)S(1)} %get-tuple-element.23), channel_id=1, source_target_pairs={{0,128},{1,129},{2,130},{3,131},{4,132},{5,133},{6,134},{7,135},{8... | collective-permute-start | bytes 122888 | tf_op jit(solution)/shard_map/ppermute | solution.py:323
  19.3 7.2 %collective-permute-start.6 = (bf16[24,2560]{1,0:T(8,128)(2,1)S(1)}, bf16[24,2560]{1,0:T(8,128)(2,1)S(1)}, u32[]{:S(2)}, u32[]{:S(2)}) collective-permute-start(bf16[24,2560]{1,0:T(8,128)(2,1)S(1)} %get-tuple-element.24), channel_id=1, source_target_pairs={{0,64},{1,65},{2,66},{3,67},{4,68},{5,69},{6,70},{7,71},{8,72},{9,... | collective-permute-start | bytes 368648 | tf_op jit(solution)/shard_map/ppermute | solution.py:323
  19.7 12.0 %collective-permute-start.3 = (bf16[2,8,2560]{2,1,0:T(8,128)(2,1)S(1)}, bf16[2,8,2560]{2,1,0:T(8,128)(2,1)S(1)}, u32[]{:S(2)}, u32[]{:S(2)}) collective-permute-start(bf16[2,8,2560]{2,1,0:T(8,128)(2,1)S(1)} %get-tuple-element.46), channel_id=1, source_target_pairs={{0,8},{1,9},{2,10},{3,11},{4,12},{5,13},{6,14},{7,15},{8,0},{9,1},... | collective-permute-start | bytes 245768 | tf_op jit(solution)/shard_map/ppermute | solution.py:323
  29.2 7.7 %collective-permute-start.11 = (bf16[4,8,2560]{2,1,0:T(8,128)(2,1)S(1)}, bf16[4,8,2560]{2,1,0:T(8,128)(2,1)S(1)}, u32[]{:S(2)}, u32[]{:S(2)}) collective-permute-start(bf16[4,8,2560]{2,1,0:T(8,128)(2,1)S(1)} %pad_maximum_fusion.5.right_a), channel_id=1, source_target_pairs={{0,48},{1,49},{2,50},{3,51},{4,52},{5,53},{6,54},{7,55},{8,56},{9,... | collective-permute-start | bytes 491528 | tf_op jit(solution)/shard_map/ppermute | solution.py:323
  31.6 9.0 %collective-permute-start.10 = (bf16[4,8,2560]{2,1,0:T(8,128)(2,1)S(1)}, bf16[4,8,2560]{2,1,0:T(8,128)(2,1)S(1)}, u32[]{:S(2)}, u32[]{:S(2)}) collective-permute-start(bf16[4,8,2560]{2,1,0:T(8,128)(2,1)S(1)} %pad_maximum_fusion.5.right_a), channel_id=1, source_target_pairs={{0,32},{1,33},{2,34},{3,35},{4,36},{5,37},{6,38},{7,39},{8,40},{9,... | collective-permute-start | bytes 491528 | tf_op jit(solution)/shard_map/ppermute | solution.py:323
  31.6 9.1 %collective-permute-start.9 = (bf16[4,8,2560]{2,1,0:T(8,128)(2,1)S(1)}, bf16[4,8,2560]{2,1,0:T(8,128)(2,1)S(1)}, u32[]{:S(2)}, u32[]{:S(2)}) collective-permute-start(bf16[4,8,2560]{2,1,0:T(8,128)(2,1)S(1)} %pad_maximum_fusion.5.right_a), channel_id=1, source_target_pairs={{0,16},{1,17},{2,18},{3,19},{4,20},{5,21},{6,22},{7,23},{8,24},{9,... | collective-permute-start | bytes 491528 | tf_op jit(solution)/shard_map/ppermute | solution.py:323
  32.4 8.4 %collective-permute-start.5 = (bf16[4,2,8,2560]{3,2,1,0:T(8,128)(2,1)S(1)}, bf16[4,2,8,2560]{3,2,1,0:T(8,128)(2,1)S(1)}, u32[]{:S(2)}, u32[]{:S(2)}) collective-permute-start(bf16[4,2,8,2560]{3,2,1,0:T(8,128)(2,1)S(1)} %pad_maximum_fusion.1.left_a), channel_id=1, source_target_pairs={{0,1},{1,0},{2,3},{3,2},{4,5},{5,4},{6,7},{7,6},{8,9},{9,8},{10,11... | collective-permute-start | bytes 983048 | tf_op jit(solution)/shard_map/ppermute | solution.py:323
  37.0 22.3 %collective-permute-start.13 = (bf16[2,16,2560]{2,1,0:T(8,128)(2,1)S(1)}, bf16[2,16,2560]{2,1,0:T(8,128)(2,1)S(1)}, u32[]{:S(2)}, u32[]{:S(2)}) collective-permute-start(bf16[2,16,2560]{2,1,0:T(8,128)(2,1)S(1)} %pad_maximum_fusion.6), channel_id=1, source_target_pairs={{0,2},{1,3},{2,0},{3,1},{4,6},{5,7},{6,4},{7,5},{8,10},{9,11},{10,... | collective-permute-start | bytes 491528 | tf_op jit(solution)/shard_map/ppermute | solution.py:323
  56.2 18.2 %collective-permute-start.12 = (bf16[2,320,128]{2,1,0:T(8,128)(2,1)S(1)}, bf16[2,320,128]{2,1,0:T(8,128)(2,1)S(1)}, u32[]{:S(2)}, u32[]{:S(2)}) collective-permute-start(bf16[2,320,128]{2,1,0:T(8,128)(2,1)S(1)} %get-tuple-element.27), channel_id=1, source_target_pairs={{0,0},{1,16},{2,32},{3,48},{4,64},{5,80},{6,96},{7,112},{8,128},{9... | collective-permute-start | bytes 491528 | tf_op jit(solution)/shard_map/ppermute | solution.py:323
  59.3 15.1 %collective-permute-start.15 = (bf16[2,2,16,2560]{3,2,1,0:T(8,128)(2,1)S(1)}, bf16[2,2,16,2560]{3,2,1,0:T(8,128)(2,1)S(1)}, u32[]{:S(2)}, u32[]{:S(2)}) collective-permute-start(bf16[2,2,16,2560]{3,2,1,0:T(8,128)(2,1)S(1)} %pad_maximum_fusion.2), channel_id=1, source_target_pairs={{0,12},{1,13},{2,14},{3,15},{4,0},{5,1},{6,2},{7,3},{8,4},{9,5},{1... | collective-permute-start | bytes 983048 | tf_op jit(solution)/shard_map/ppermute | solution.py:323
  63.7 13.3 %collective-permute-start.14 = (bf16[2,2,16,2560]{3,2,1,0:T(8,128)(2,1)S(1)}, bf16[2,2,16,2560]{3,2,1,0:T(8,128)(2,1)S(1)}, u32[]{:S(2)}, u32[]{:S(2)}) collective-permute-start(bf16[2,2,16,2560]{3,2,1,0:T(8,128)(2,1)S(1)} %pad_maximum_fusion.2), channel_id=1, source_target_pairs={{0,4},{1,5},{2,6},{3,7},{4,8},{5,9},{6,10},{7,11},{8,12},{9,13},{1... | collective-permute-start | bytes 983048 | tf_op jit(solution)/shard_map/ppermute | solution.py:323
  77.0 13.8 %collective-permute-start.18 = (bf16[320,128]{1,0:T(8,128)(2,1)S(1)}, bf16[320,128]{1,0:T(8,128)(2,1)S(1)}, u32[]{:S(2)}, u32[]{:S(2)}) collective-permute-start(bf16[320,128]{1,0:T(8,128)(2,1)S(1)} %get-tuple-element.44), channel_id=1, source_target_pairs={{0,192},{1,193},{2,194},{3,195},{4,196},{5,197},{6,198},{7,199},{8... | collective-permute-start | bytes 245768 | tf_op jit(solution)/shard_map/ppermute | solution.py:323
  77.1 13.7 %collective-permute-start.16 = (bf16[320,128]{1,0:T(8,128)(2,1)S(1)}, bf16[320,128]{1,0:T(8,128)(2,1)S(1)}, u32[]{:S(2)}, u32[]{:S(2)}) collective-permute-start(bf16[320,128]{1,0:T(8,128)(2,1)S(1)} %get-tuple-element.44), channel_id=1, source_target_pairs={{0,64},{1,65},{2,66},{3,67},{4,68},{5,69},{6,70},{7,71},{8,72},{9,... | collective-permute-start | bytes 245768 | tf_op jit(solution)/shard_map/ppermute | solution.py:323
  83.9 6.9 %collective-permute-start.17 = (bf16[320,128]{1,0:T(8,128)(2,1)S(1)}, bf16[320,128]{1,0:T(8,128)(2,1)S(1)}, u32[]{:S(2)}, u32[]{:S(2)}) collective-permute-start(bf16[320,128]{1,0:T(8,128)(2,1)S(1)} %get-tuple-element.43), channel_id=1, source_target_pairs={{0,128},{1,129},{2,130},{3,131},{4,132},{5,133},{6,134},{7,135},{8... | collective-permute-start | bytes 245768 | tf_op jit(solution)/shard_map/ppermute | solution.py:323
  84.0 6.9 %collective-permute-start.20 = (bf16[2,16,2560]{2,1,0:T(8,128)(2,1)S(1)}, bf16[2,16,2560]{2,1,0:T(8,128)(2,1)S(1)}, u32[]{:S(2)}, u32[]{:S(2)}) collective-permute-start(bf16[2,16,2560]{2,1,0:T(8,128)(2,1)S(1)} %slice_bitcast_fusion), channel_id=1, source_target_pairs={{0,12},{1,13},{2,14},{3,15},{4,0},{5,1},{6,2},{7,3},{8,4},{9,5},{1... | collective-permute-start | bytes 491528 | tf_op jit(solution)/shard_map/ppermute | solution.py:323
  84.6 6.3 %collective-permute-start.19 = (bf16[2,16,2560]{2,1,0:T(8,128)(2,1)S(1)}, bf16[2,16,2560]{2,1,0:T(8,128)(2,1)S(1)}, u32[]{:S(2)}, u32[]{:S(2)}) collective-permute-start(bf16[2,16,2560]{2,1,0:T(8,128)(2,1)S(1)} %slice_bitcast_fusion.1), channel_id=1, source_target_pairs={{0,4},{1,5},{2,6},{3,7},{4,8},{5,9},{6,10},{7,11},{8,12},{9,13},{1... | collective-permute-start | bytes 491528 | tf_op jit(solution)/shard_map/ppermute | solution.py:323
  91.1 22.0 %collective-permute-start.25 = (bf16[4,2,2,16,2560]{4,3,2,1,0:T(8,128)(2,1)S(1)}, bf16[4,2,2,16,2560]{4,3,2,1,0:T(8,128)(2,1)S(1)}, u32[]{:S(2)}, u32[]{:S(2)}) collective-permute-start(bf16[4,2,2,16,2560]{4,3,2,1,0:T(8,128)(2,1)S(1)} %pad_maximum_fusion.everyone_a), channel_id=1, source_target_pairs={{0,1},{1,0},{2,3},{3,2},{4,5},{5,4},{6,7},{7,6},{8,9},{9,8},{10,11... | collective-permute-start | bytes 3932168 | tf_op jit(solution)/shard_map/ppermute | solution.py:323
  92.7 10.8 %collective-permute-start.23 = (bf16[4,320,128]{2,1,0:T(8,128)(2,1)S(1)}, bf16[4,320,128]{2,1,0:T(8,128)(2,1)S(1)}, u32[]{:S(2)}, u32[]{:S(2)}) collective-permute-start(bf16[4,320,128]{2,1,0:T(8,128)(2,1)S(1)} %pad_maximum_fusion.3.part_a), channel_id=1, source_target_pairs={{0,48},{1,49},{2,50},{3,51},{4,52},{5,53},{6,54},{7,55},{8,56},{9,... | collective-permute-start | bytes 983048 | tf_op jit(solution)/shard_map/ppermute | solution.py:323
  96.4 10.6 %collective-permute-start.21 = (bf16[4,320,128]{2,1,0:T(8,128)(2,1)S(1)}, bf16[4,320,128]{2,1,0:T(8,128)(2,1)S(1)}, u32[]{:S(2)}, u32[]{:S(2)}) collective-permute-start(bf16[4,320,128]{2,1,0:T(8,128)(2,1)S(1)} %pad_maximum_fusion.3.part_a), channel_id=1, source_target_pairs={{0,16},{1,17},{2,18},{3,19},{4,20},{5,21},{6,22},{7,23},{8,24},{9,... | collective-permute-start | bytes 983048 | tf_op jit(solution)/shard_map/ppermute | solution.py:323
  103.5 6.1 %collective-permute-start.24 = (bf16[2,320,128]{2,1,0:T(8,128)(2,1)S(1)}, bf16[2,320,128]{2,1,0:T(8,128)(2,1)S(1)}, u32[]{:S(2)}, u32[]{:S(2)}) collective-permute-start(bf16[2,320,128]{2,1,0:T(8,128)(2,1)S(1)} %slice.41), channel_id=1, source_target_pairs={{0,48},{1,49},{2,50},{3,51},{4,52},{5,53},{6,54},{7,55},{8,56},{9,... | collective-permute-start | bytes 491528 | tf_op jit(solution)/shard_map/ppermute | solution.py:323
  107.0 6.1 %collective-permute-start.22 = (bf16[2,320,128]{2,1,0:T(8,128)(2,1)S(1)}, bf16[2,320,128]{2,1,0:T(8,128)(2,1)S(1)}, u32[]{:S(2)}, u32[]{:S(2)}) collective-permute-start(bf16[2,320,128]{2,1,0:T(8,128)(2,1)S(1)} %slice.40), channel_id=1, source_target_pairs={{0,16},{1,17},{2,18},{3,19},{4,20},{5,21},{6,22},{7,23},{8,24},{9,... | collective-permute-start | bytes 491528 | tf_op jit(solution)/shard_map/ppermute | solution.py:323
  (13 other events, 245.1 us)
